TPU v7x, 128 devices: a whole 4x4x4 slice. The times are simulated.
128 devices in a mesh: sfc: 16 (over y, x), grp: 8 (over z, core).
Axes of the slice: x: 4, y: 4, z: 4, core: 2. Of those that a mesh axis runs over, the one named last changes fastest.
Arguments:
- bin_points: float32 [131072, 5, 256], P(('sfc', 'grp')), may hold values from -1 to 1, as said below
- bin_plan: int32 [131072, 1], P(('sfc', 'grp')), may hold values from 0 to 15; in each aligned block of 1024 rows (0 to 1023, 1024 to 2047, ...) at most 128 rows name the same one
- bin_leaf: int32 [131072], P(('sfc', 'grp')), may hold values from 0 to 255
- leaf_slots: int32 [16, 8, 256], P('sfc', None, 'grp'), may hold values from 0 to 255, each once within a row
- box_slots: int32 [16, 8, 32], P('sfc'), may hold values from 0 to 31, each once within a row
- parent_cone: int32 [16, 256], P('sfc'), may hold values from 0 to 15
- box_cone: int32 [16, 32], P('sfc'), may hold values from 0 to 15
- cone_angles: float32 [16, 2], replicated, may hold values from -3.140625 to 3.140625
Outputs:
- leaf_expansions: float32 [32768, 2, 512], P(('sfc', 'grp'))
- level_one: float32 [4096, 2, 512], P(('sfc', 'grp'))
- level_two: float32 [512, 2, 512], P(('sfc', 'grp'))
Inputs may be any that keep to these rules, and one draw needn't show every extreme that they name: `bin_plan`: among the rows of one device no value is named by more than 128 rows, a bound that some block reaches. Each row leaf_slots[s, o, :] names every level-one box of segment s once, so every level-one box has exactly one child of each octant. Each row box_slots[s, o, :] names every level-two box of segment s once. `bin_points`: coordinates lie within -1 to 1 and densities within -0.4 to 0.4.
All inputs are finite; a program needn't handle non-finite values.
Results may differ from a plain program's by a relative error of at most 0.0039.
Values sent between devices are 32-bit elements; how exact they have to be, the bound alone decides.
No kernel may reach another device: no remote copies, remote signals or barrier semaphores. Data moves between devices by JAX's collectives and lax.ppermute only.
A program may use at most 320 MiB of HBM per device.

v0:
```python
import functools

import jax
import jax.numpy as jnp
import numpy as np
from jax import lax
from jax.experimental import pallas as pl
from jax.experimental.pallas import tpu as pltpu
from jax.sharding import PartitionSpec as P

kappa_leaf = 2.0
kappa_box = 4.0
f32 = jnp.float32
i32 = jnp.int32
VMEM = pl.BlockSpec(memory_space=pltpu.VMEM)
SMEM = pl.BlockSpec(memory_space=pltpu.SMEM)
ANY = pl.BlockSpec(memory_space=pl.ANY)


def cheb_nodes():
    return np.cos((2.0 * np.arange(8) + 1.0) * np.pi / 16.0)


def lagrange_np(values):
    nodes = cheb_nodes()
    rows = []
    for center in range(8):
        weight = np.ones_like(values)
        for other in range(8):
            if other != center:
                weight = weight * (values - nodes[other]) / (nodes[center] - nodes[other])
        rows.append(weight)
    return np.stack(rows, axis=0)


def child_axis(bit):
    return 0.5 * (2 * bit - 1) + 0.5 * cheb_nodes()


def axis_maps():
    return np.stack([lagrange_np(child_axis(bit)) for bit in range(2)])


def tile_of_nodes(first, second, third):
    rows = np.arange(8)[:, None]
    lanes = np.arange(128)[None, :]
    a = 2 * (rows // 2) + lanes // 64
    b = lanes % 64 // 8 + 0 * rows
    c = lanes % 8 + 0 * rows
    return np.stack([first[a], second[b], third[c]])


def lane_maps():
    maps = axis_maps()
    out = []
    for pick in range(4):
        both = np.kron(maps[pick // 2], maps[pick % 2])
        full = np.kron(np.eye(2), both).T
        high = full.astype(jnp.bfloat16)
        low = (full - high.astype(np.float64)).astype(jnp.bfloat16)
        out.append(np.block([[high, low], [high, np.zeros_like(low)]]))
    return np.stack(out).astype(jnp.bfloat16)


def row_maps():
    maps = axis_maps()
    rows = np.arange(8)[:, None]
    half = np.arange(128)[None, :] // 64
    k = rows // 2
    out = np.zeros((2, 8, 8, 128), np.float32)
    for bit in range(2):
        for step in range(4):
            for flip in range(2):
                to = 2 * k + half
                frm = 2 * ((k + step) % 4) + (half ^ flip)
                out[bit, 2 * step + flip] = maps[bit][to, frm]
    return out


def basis(x):
    t = cheb_nodes()[:4]
    sq = t * t
    x2 = x * x
    s = [x2 - float(v) for v in sq]
    p01 = s[0] * s[1]
    p23 = s[2] * s[3]
    rest = [s[1] * p23, s[0] * p23, p01 * s[3], p01 * s[2]]
    out = [None] * 8
    for j in range(4):
        scale = 1.0 / (np.prod([sq[j] - sq[i] for i in range(4) if i != j]) * 2.0 * t[j])
        q = rest[j] * float(scale)
        out[j] = q * (x + float(t[j]))
        out[7 - j] = q * (float(t[j]) - x)
    return out


def lanes_of(shape):
    return lax.broadcasted_iota(i32, shape, len(shape) - 1)


def lanes_of(shape):
    return lax.broadcasted_iota(i32, shape, len(shape) - 1)


CHUNKS = ((2, 1), (3, 0))
ORDER = tuple(m for chunk in CHUNKS for m in chunk)


def route_kernel(here, plan, leaf, table, labels, picked, scaled):
    bf16 = jnp.bfloat16
    cap = labels.shape[2]
    target = plan[...]
    names = leaf[...].astype(f32)
    along_x = (target - here[0]) % 4
    along_y = (target // 4 - here[1]) % 4
    first = jnp.where(here[2] == 0, along_x, along_y)
    second = jnp.where(here[2] == 0, along_y, along_x)
    place, lead, width, part_of = target * 0, target * 0, target * 0, target * 0
    for c, chunk in enumerate(CHUNKS):
        for n, m in enumerate(chunk):
            hit = second == m
            place = jnp.where(hit, ORDER.index(m), place)
            part_of = jnp.where(hit, c, part_of)
            lead = jnp.where(hit, n, lead)
            width = jnp.where(hit, len(chunk), width)
    code = place * 4 + first
    for d in range(16):
        hit = (code == d).astype(f32)
        picked[pl.ds(8 * d, 8), :] = hit
        scaled[pl.ds(8 * d, 8), :] = hit * names
    square = (128, 128)
    row, lane = rows_of(square), lanes_of(square)
    hits = picked[...].astype(bf16)
    ones = jnp.ones(square, bf16)

    def mul(a, b):
        return jnp.dot(a.astype(bf16), b.astype(bf16), preferred_element_type=f32)

    inside = mul(hits, (row < lane).astype(f32))
    ahead = mul(mul((lane < row).astype(f32), hits), ones)
    same = mul(mul(((lane < row) & (lane // 8 == row // 8)).astype(f32), hits), ones)
    order = jnp.zeros((8, 128), f32)
    slot = jnp.zeros((8, 128), f32)
    for d in range(16):
        part = slice(8 * d, 8 * d + 8)
        hit = picked[pl.ds(8 * d, 8), :]
        order = order + hit * (inside[part] + ahead[part])
        slot = slot + hit * (inside[part] + same[part])
    count = ENTRIES
    lane_w = lanes_of((1, count))
    spans = jnp.zeros((1, count), f32)
    start = jnp.zeros((1, 1), f32)
    before = jnp.zeros((1, 1), f32)
    for c in range(len(CHUNKS)):
        size = jnp.sum((part_of == c).astype(f32), keepdims=True)
        groups = jnp.floor((size + float(GROUP - 1)) * (1.0 / GROUP))
        spans = jnp.where(lane_w == 2 * c, jnp.broadcast_to(start, (1, count)), spans)
        spans = jnp.where(lane_w == 2 * c + 1, jnp.broadcast_to(groups, (1, count)), spans)
        order = order + jnp.where(
            part_of == c, jnp.broadcast_to(start - before, order.shape), 0.0
        )
        start = start + groups * float(GROUP)
        before = before + size
    goal_hi = (first * width + lead).astype(f32)
    ranks = lax.broadcasted_iota(i32, (count, 128), 0).astype(f32)
    seats = row.astype(f32)
    sub = lax.broadcasted_iota(i32, (8, 128), 0)
    lane_f = lanes_of((8, 128)).astype(f32)
    found = jnp.zeros((8, count), f32)
    marks = jnp.zeros((32, 128), f32)
    nt = (((1,), (1,)), ((), ()))
    for r in range(8):
        at = jnp.broadcast_to(order[r : r + 1, :], (count, 128)) == ranks
        goal = jnp.broadcast_to(goal_hi[r : r + 1, :], (8, 128))
        seat = jnp.broadcast_to(slot[r : r + 1, :], (8, 128))
        values = jnp.where(
            sub == 0, 2.0 * lane_f - (lanes_of((8, 128)) % 8).astype(f32),
            jnp.where(sub == 1, float(r), jnp.where(sub == 2, goal, jnp.where(sub == 3, seat, 1.0))),
        )
        found = found + lax.dot_general(
            values.astype(bf16), at.astype(f32).astype(bf16), nt, preferred_element_type=f32
        )
        both = jnp.concatenate(
            [scaled[pl.ds(r, 16, stride=8), :], picked[pl.ds(r, 16, stride=8), :]], axis=0
        )
        sits = jnp.broadcast_to(slot[r : r + 1, :], square) == seats
        marks = marks + lax.dot_general(
            both.astype(bf16), sits.astype(f32).astype(bf16), nt, preferred_element_type=f32
        )
    lines = (found[0:1] + found[1:2] * 256.0).astype(i32)
    goals = (found[2:3] * float(cap_rows(cap)) + found[3:4] + found[4:5]).astype(i32)
    for n, values in enumerate((lines, goals)):
        for r in range(count // 128):
            at = n * (count // 128) + r
            table[at : at + 1, :] = values[:, 128 * r : 128 * r + 128]
    at = 2 * (count // 128)
    table[at : at + 1, :] = spans[:, :128].astype(i32)
    label = marks[:16] + 256.0 * (1.0 - marks[16:])
    for d in range(16):
        total = jnp.sum(marks[16 + d : 17 + d], axis=1, keepdims=True)
        labels[d] = jnp.where(
            sub == 0,
            jnp.broadcast_to(label[d : d + 1], (8, 128)),
            jnp.broadcast_to(total, (8, 128)),
        )


def cap_rows(cap):
    return cap + 1


def route(here, plan, leaf):
    bins = plan.shape[0]
    return pl.pallas_call(
        route_kernel,
        out_shape=(
            jax.ShapeDtypeStruct((24, 128), i32),
            jax.ShapeDtypeStruct((16, 8, 128), f32),
        ),
        in_specs=[SMEM, VMEM, VMEM],
        out_specs=(VMEM, VMEM),
        scratch_shapes=[pltpu.VMEM((128, 128), f32)] * 2,
        name="route",
    )(here, plan.reshape(bins // 128, 128), leaf.reshape(bins // 128, 128))


GROUP = 16
ENTRIES = 1152


def expand_kernel(chunk, table, labels, pts, *refs):
    outs = refs[:4]
    held, all_pts = refs[4:6]
    stage, bx, by, bz, sems, load_sems = refs[6:]
    first = sum(len(c) for c in CHUNKS[:chunk])
    wide = len(CHUNKS[chunk])
    rows = outs[0].shape[1]
    cap = rows - 1
    span = all_pts.shape[0] // 5
    loads = [
        pltpu.make_async_copy(
            pts.at[pl.ds(span * axis, span)], all_pts.at[pl.ds(span * axis, span)],
            load_sems.at[axis],
        )
        for axis in range(5)
    ]
    for load in loads:
        load.start()
    for k in range(4):
        for n in range(wide):
            held[1 + (k * wide + n) * rows + cap] = labels[4 * (first + n) + k]
    begin = table[2 * ENTRIES + 2 * chunk]
    trips = table[2 * ENTRIES + 2 * chunk + 1]
    for load in loads:
        load.wait()

    def fetch(g, u, bank):
        line = table[begin + g * GROUP + u]
        for axis in range(3):
            for h in range(2):
                stage[bank, axis, h, pl.ds(u, 1), :] = all_pts[
                    pl.ds(line + (span * axis + 8 * h), 1), :
                ]

    def tabulate(piece, bank):
        u, h, axis = 8 * (piece // 6), piece // 3 % 2, piece % 3
        values = basis(stage[bank, axis, h, pl.ds(u, 8), :])
        for a in range(8):
            if axis == 1:
                by[bank, h, pl.ds(GROUP * a + u, 8), :] = values[a]
            else:
                ref = bz if axis else bx
                ref[bank, h, pl.ds(8 * u + a, 8, stride=8), :] = values[a]

    def consume(g, u, bank):
        base = begin + g * GROUP
        line = table[base + u]
        weighted, pair = [], []
        for h in range(2):
            lx = bx[bank, h, pl.ds(8 * u, 8), :]
            lz = bz[bank, h, pl.ds(8 * u, 8), :]
            re, im = (
                jnp.broadcast_to(
                    all_pts[pl.ds(line + (span * (3 + part) + 8 * h), 1), :], lx.shape
                )
                for part in range(2)
            )
            weighted.append(jnp.concatenate([re * lx, im * lx], axis=0).astype(jnp.bfloat16))
            pair.append(
                jnp.concatenate(
                    [
                        jnp.broadcast_to(by[bank, h, pl.ds(GROUP * b + u, 1), :], lz.shape) * lz
                        for b in range(8)
                    ],
                    axis=0,
                ).astype(jnp.bfloat16)
            )
        res = lax.dot_general(
            jnp.concatenate(weighted, axis=1),
            jnp.concatenate(pair, axis=1),
            (((1,), (1,)), ((), ())),
            preferred_element_type=f32,
        )
        held[table[base + (ENTRIES + u)]] = jnp.concatenate([res[:8], res[8:]], axis=1)

    pieces = 6 * GROUP // 8
    for u in range(GROUP):
        fetch(0, u, 0)
    for piece in range(pieces):
        tabulate(piece, 0)
    for u in range(GROUP):
        fetch(1, u, 1)

    def step(g, carry):
        bank = g & 1
        for u in range(GROUP):
            consume(g, u, bank)
            if u % 4 == 3:
                for piece in range(3 * (u // 4), 3 * (u // 4) + 3):
                    tabulate(piece, 1 - bank)
                for v in range(u - 3, u + 1):
                    fetch(g + 2, v, bank)
        return carry

    lax.fori_loop(0, trips, step, 0)
    copies = []
    for k in range(4):
        for n in range(wide):
            copies.append(
                pltpu.make_async_copy(
                    held.at[pl.ds(1 + (k * wide + n) * rows, rows)], outs[k].at[n], sems.at[k, n]
                )
            )
    for copy in copies:
        copy.start()
    for copy in copies:
        copy.wait()


def expand(chunk, table, labels, pts, cap):
    wide = len(CHUNKS[chunk])
    return pl.pallas_call(
        functools.partial(expand_kernel, chunk),
        out_shape=[jax.ShapeDtypeStruct((wide, cap + 1, 8, 128), f32)] * 4,
        in_specs=[SMEM, VMEM, ANY],
        out_specs=[ANY] * 4,
        scratch_shapes=[
            pltpu.VMEM((4 * wide * (cap + 1) + 1, 8, 128), f32),
            pltpu.VMEM(pts.shape, f32),
            pltpu.VMEM((2, 3, 2, GROUP, 128), f32),
            *[pltpu.VMEM((2, 2, 8 * GROUP, 128), f32)] * 3,
            pltpu.SemaphoreType.DMA((4, wide)),
            pltpu.SemaphoreType.DMA((5,)),
        ],
        cost_estimate=pl.CostEstimate(
            flops=wide * (1 << 28), bytes_accessed=1 << 23, transcendentals=0
        ),
        name="expand",
    )(table, labels, pts)


def gather_kernel(wide, *refs):
    arrived, outs = refs[:4], refs[4 : 4 + wide]
    held, labels, names, sem, sems = refs[4 + wide :]
    cap = held.shape[2] - 1
    loads = [pltpu.make_async_copy(arrived[k], held.at[k], sems.at[k]) for k in range(4)]
    for load in loads:
        load.start()
    for out in outs:
        out[...] = jnp.zeros(out.shape, f32)
    for load in loads:
        load.wait()
    for k in range(4):
        for n in range(wide):
            labels[pl.ds(8 * (k * wide + n), 8), :] = held[k, n, cap].astype(i32)
    copy = pltpu.make_async_copy(labels, names, sem)
    copy.start()
    copy.wait()
    for k in range(4):
        most = names[8 * k * wide + 1, 0]
        for n in range(1, wide):
            most = jnp.maximum(most, names[8 * (k * wide + n) + 1, 0])

        def rows4(r, carry):
            for u in range(4):
                for n in range(wide):
                    slot = r * 4 + u
                    where = names[8 * (k * wide + n), slot]
                    outs[n][where] = outs[n][where] + held[k, n, slot]
            return carry

        lax.fori_loop(0, (most + 3) // 4, rows4, 0)


def gather(arrived, leaf_count):
    wide, rows = arrived[0].shape[:2]
    return pl.pallas_call(
        functools.partial(gather_kernel, wide),
        out_shape=[jax.ShapeDtypeStruct((leaf_count + 1, 8, 128), f32)] * wide,
        in_specs=[pl.BlockSpec(memory_space=pl.ANY)] * 4,
        out_specs=[VMEM] * wide,
        scratch_shapes=[
            pltpu.VMEM((4, wide, rows, 8, 128), f32),
            pltpu.VMEM((32 * wide, 128), i32),
            pltpu.SMEM((32 * wide, 128), i32),
            pltpu.SemaphoreType.DMA(()),
            pltpu.SemaphoreType.DMA((4,)),
        ],
        cost_estimate=pl.CostEstimate(
            flops=wide * (1 << 26), bytes_accessed=wide << 22, transcendentals=0
        ),
        name="gather",
    )(*arrived)


def rows_of(shape):
    return lax.broadcasted_iota(i32, shape, len(shape) - 2)


def swap_rows(t):
    even = rows_of(t.shape) % 2 == 0
    axis = len(t.shape) - 2
    return jnp.where(even, pltpu.roll(t, 7, axis), pltpu.roll(t, 1, axis))


def spin(t, cosine, sine):
    return t * cosine + swap_rows(t) * sine


def row_mix(t, maps, bit):
    flipped = pltpu.roll(t, 64, 2)
    total = None
    for step in range(4):
        for flip in range(2):
            part = flipped if flip else t
            if step:
                part = pltpu.roll(part, 8 - 2 * step, 1)
            term = part * maps[bit, 2 * step + flip]
            total = term if total is None else total + term
    return total


SEATS = 36


def phases_kernel(
    here, slots, boxes, cones, box_cones, e0c, e0s, e1c, e1s, e2c, e2s, p0c, p0s, p1c, p1s, goal
):
    side = here[2]
    for o in range(8):

        def child(j, carry):
            p = slots[o, j]
            e = cones[p] * 8 + o
            p0c[o, j] = e0c[e]
            p0s[o, j] = e0s[e]
            owner = p >> 5
            goal[o, j] = ((((owner & 1) ^ side) << 2) + (owner >> 1)) * SEATS + (p & 31)
            q = boxes[o, j]
            a = cones[8 * j + o]
            b = box_cones[q] * 8 + o
            ca, sa, cb, sb = e1c[a], e1s[a], e2c[b], e2s[b]
            p1c[o, j] = ca * cb - sa * sb
            p1s[o, j] = sa * cb + ca * sb
            owner = q >> 2
            goal[8 + o, j] = ((((owner & 1) ^ side) << 2) + (owner >> 1)) * SEATS + 32 + (q & 3)
            return carry

        lax.fori_loop(0, 32, child, 0, unroll=4)


def translate(t, both, rows, octant):
    count = t.shape[0]
    flat = t.reshape(count * 8, 128)
    high = flat.astype(jnp.bfloat16)
    low = (flat - high.astype(f32)).astype(jnp.bfloat16)
    res = jnp.dot(
        jnp.concatenate([high, low], axis=1), both[octant % 4], preferred_element_type=f32
    )
    return row_mix((res[:, :128] + res[:, 128:]).reshape(count, 8, 128), rows, octant // 4)


def levels_kernel(
    here, goal, a0, a1, a2, a3, p0c, p0s, p1c, p1s, both, rows, leaves, mine, other, acc, moved
):
    acc[...] = jnp.zeros(acc.shape, f32)
    step = 16
    shape = (step, 8, 128)
    own = rows_of(shape) % 2 == lanes_of(shape) // 64

    def settle(n, carry):
        base = pl.multiple_of(n * step, step)
        t = (a0[pl.ds(base, step)] + a1[pl.ds(base, step)]) + (
            a2[pl.ds(base, step)] + a3[pl.ds(base, step)]
        )
        leaves[pl.ds(base, step)] = jnp.where(own, t, swap_rows(pltpu.roll(t, 64, 2)))
        return carry

    lax.fori_loop(0, leaves.shape[0] // step, settle, 0)

    def spread(o, lead):
        for start in range(0, 32, 8):
            spots = [goal[lead + o, start + j] for j in range(8)]
            sums = [acc[spots[j]] + moved[o % 2, start + j] for j in range(8)]
            for j in range(8):
                acc[spots[j]] = sums[j]

    for o in range(8):
        for part in range(0, 32, 8):
            t = jnp.stack([leaves[8 * (part + j) + o] for j in range(8)])
            t = spin(t, p0c[o, part : part + 8], p0s[o, part : part + 8])
            moved[o % 2, part : part + 8] = translate(t, both, rows, o)
        spread(o, 0)

    apart = [here[2] * 4 * SEATS, (1 - here[2]) * 4 * SEATS]
    for o in range(8):
        for part in range(0, 32, 8):
            tiles = []
            for j in range(8):
                p = 8 * (part + j) + o
                owner = p // 32
                tiles.append(acc[(owner // 2) * SEATS + p % 32 + apart[owner % 2]])
            t = spin(jnp.stack(tiles), p1c[o, part : part + 8], p1s[o, part : part + 8])
            moved[o % 2, part : part + 8] = translate(t, both, rows, o)
        spread(o, 8)
    for z in range(4):
        mine[z] = acc[pl.ds(z * SEATS, SEATS)]
        other[z] = acc[pl.ds((4 + z) * SEATS, SEATS)]


def merge_kernel(here, mine, got, *outs):
    for k in range(4):
        z = (here[3] + k) % 4
        outs[k][...] = mine[z] + got[z]


def close_kernel(here, cones, box_cones, g0, g1, g2, g3, e1c, e1s, e3c, e3s, out_one, out_two):
    owned, upper = out_one.shape[0], out_two.shape[0]
    me = 2 * here[3] + here[2]
    for n in range(SEATS):
        t = (g0[n] + g1[n]) + (g2[n] + g3[n])
        if n < owned:
            e = cones[me * owned + n]
            out_one[n] = spin(t, e1c[e], e1s[e])
        else:
            e = box_cones[me * upper + n - owned]
            out_two[n - owned] = spin(t, e3c[e], e3s[e])


def phase_tables(directions, kappa, places):
    grid = jnp.asarray(places.astype(np.float32))
    angle = (
        directions[:, 0, None, None, None] * grid[None, :, 0]
        + directions[:, 1, None, None, None] * grid[None, :, 1]
        + directions[:, 2, None, None, None] * grid[None, :, 2]
    )
    angle = (kappa * angle).reshape(-1, 8, 128)
    sign = jnp.where(lax.broadcasted_iota(i32, (1, 8, 128), 1) % 2 == 0, -1.0, 1.0).astype(f32)
    return jnp.cos(angle), jnp.sin(angle) * sign


def to_nodes(tiles):
    count = tiles.shape[0]
    return tiles.reshape(count, 4, 2, 128).transpose(0, 2, 1, 3).reshape(count, 2, 512)


def cone_vectors(cone_angles):
    azimuth = cone_angles[:, 0]
    polar = cone_angles[:, 1]
    return jnp.stack(
        [jnp.cos(azimuth) * jnp.sin(polar), jnp.sin(azimuth) * jnp.sin(polar), jnp.cos(polar)],
        axis=1,
    )


def hop(x, shift, leg, groups):
    pairs = []
    for s in range(16):
        for g in range(groups):
            y, x0 = s // 4, s % 4
            if g % 2 == leg:
                x0 = (x0 + shift) % 4
            else:
                y = (y + shift) % 4
            pairs.append((s * groups + g, (4 * y + x0) * groups + g))
    return lax.ppermute(x, ("sfc", "grp"), pairs)


def around(x, shift, groups):
    pairs = [(g, (g + 2 * shift) % groups) for g in range(groups)]
    return lax.ppermute(x, "grp", pairs)


def after(value, *others):
    return lax.optimization_barrier((value, *others))[0]


def per_device(
    bin_points, bin_plan, bin_leaf, leaf_slots, box_slots, parent_cone, box_cone, cone_angles
):
    groups = lax.axis_size("grp")
    rank = lax.axis_index("grp")
    cap = bin_points.shape[0] // 8
    leaf_count = leaf_slots.shape[2] * 8
    first_owned = parent_cone.shape[1] // groups
    second_owned = box_cone.shape[1] // groups
    tile = jax.ShapeDtypeStruct((8, 128), f32)

    def tiles(*lead):
        return jax.ShapeDtypeStruct((*lead, *tile.shape), f32)

    me = lax.axis_index("sfc")
    here = jnp.stack([me % 4, me // 4, rank % 2, rank // 2]).astype(i32)
    table, labels = route(here, bin_plan[:, 0], bin_leaf)
    table = table.reshape(-1)
    bins, _, width = bin_points.shape
    pts = jnp.transpose(bin_points.reshape(bins // 8, 8, 5, width // 128, 128), (2, 0, 3, 1, 4))
    pts = pts.reshape(-1, 128)
    arrived = []
    for c in range(len(CHUNKS)):
        sent = expand(c, table, labels, pts, cap)
        table = after(table, sent[0])
        moved = [sent[0]]
        for k in (2, 1, 3):
            moved.append(hop(sent[k], k, 0, groups))
        arrived.append(moved)

    cone_angles = after(cone_angles, sent[0])
    directions = cone_vectors(cone_angles)
    child = np.stack(
        [
            tile_of_nodes(child_axis(o // 4), child_axis(o // 2 % 2), child_axis(o % 2))
            for o in range(8)
        ]
    )
    nodes = cheb_nodes()
    parent = tile_of_nodes(nodes, nodes, nodes)[None]
    e0c, e0s = phase_tables(directions, kappa_leaf, child)
    e1c, e1s = phase_tables(directions, -kappa_leaf, parent)
    e2c, e2s = phase_tables(directions, kappa_box, child)
    e3c, e3s = phase_tables(directions, -kappa_box, parent)
    make_phases = pl.pallas_call(
        phases_kernel,
        out_shape=(tiles(8, 32),) * 4 + (jax.ShapeDtypeStruct((16, 32), i32),),
        in_specs=[SMEM] * 5 + [VMEM] * 6,
        out_specs=(VMEM,) * 4 + (SMEM,),
        name="phases",
    )
    p0c, p0s, p1c, p1s, goal = make_phases(
        here, leaf_slots[0], box_slots[0], parent_cone[0], box_cone[0],
        e0c, e0s, e1c, e1s, e2c, e2s,
    )

    held = [None] * 4
    last = sent[0]
    for c, chunk in enumerate(CHUNKS):
        got = [after(arrived[c][0], last)] + arrived[c][1:]
        sums = gather(got, leaf_count)
        last = sums[0]
        for m, part in zip(chunk, sums):
            held[m] = hop(part, m, 1, groups) if m else part

    leaves, mine, other = pl.pallas_call(
        levels_kernel,
        out_shape=(tiles(leaf_count), tiles(4, SEATS), tiles(4, SEATS)),
        in_specs=[SMEM] * 2 + [VMEM] * 10,
        out_specs=(VMEM,) * 3,
        scratch_shapes=[
            pltpu.VMEM((8 * SEATS, 8, 128), f32),
            pltpu.VMEM((2, 32, 8, 128), f32),
        ],
        name="levels",
    )(
        here, goal, *held, p0c, p0s, p1c, p1s,
        jnp.asarray(lane_maps()), jnp.asarray(row_maps()),
    )
    swapped = lax.ppermute(other, "grp", [(g, g ^ 1) for g in range(groups)])
    blocks = pl.pallas_call(
        merge_kernel,
        out_shape=(tiles(SEATS),) * 4,
        in_specs=[SMEM] + [VMEM] * 2,
        out_specs=(VMEM,) * 4,
        name="merge",
    )(here, mine, swapped)
    got = [blocks[0]] + [around(blocks[k], k, groups) for k in (1, 2, 3)]
    one, two = pl.pallas_call(
        close_kernel,
        out_shape=(tiles(first_owned), tiles(second_owned)),
        in_specs=[SMEM] * 3 + [VMEM] * 8,
        out_specs=(VMEM, VMEM),
        name="close",
    )(here, parent_cone[0], box_cone[0], *got, e1c, e1s, e3c, e3s)
    return (to_nodes(leaves), to_nodes(one), to_nodes(two))


def solution(mesh):
    placed = (
        P(("sfc", "grp"), None, None),
        P(("sfc", "grp"), None),
        P(("sfc", "grp")),
        P("sfc", None, "grp"),
        P("sfc", None, None),
        P("sfc", None),
        P("sfc", None),
        P(),
    )

    return jax.shard_map(
        per_device,
        mesh=mesh,
        in_specs=placed,
        out_specs=(
            P(("sfc", "grp"), None, None),
            P(("sfc", "grp"), None, None),
            P(("sfc", "grp"), None, None),
        ),
        check_vma=False,
    )
```

profile of v0, /device:TPU:0, one launch (start us, length us, event | category | flops | bytes accessed | tf_op | source)
XLA Modules:
  0.0 156.0 jit_solution(9647637712933665885)
XLA Ops:
  0.7 0.6 pad_add_fusion.here
  1.3 2.7 %route.1 = (s32[24,128]{1,0:T(8,128)}, f32[16,8,128]{2,1,0:T(8,128)}) custom-call(s32[4]{0:T(128)} %pad_add_fusion.here, s32[8,128]{1,0:T(8,128)} %bitcast.107, s32[8,128]{1,0:T(8,128)} %bitcast.108), custom_call_target="tpu_custom_call" | custom-call | tf_op jit(solution)/shard_map/route/pallas_call | solution.py:214
  4.0 19.7 %expand.2 = (f32[2,129,8,128]{3,2,1,0:T(8,128)}, f32[2,129,8,128]{3,2,1,0:T(8,128)}, f32[2,129,8,128]{3,2,1,0:T(8,128)}, f32[2,129,8,128]{3,2,1,0:T(8,128)}) custom-call(s32[3072]{0:T(1024)} %bitcast.101, f32[16,8,128]{2,1,0:T(8,128)} %get-tuple-element.36.labels, f32[10240,128]{1,0:T(8,128)} %bitcast.99), custom_call_target="tpu_custom_call" | custom-call | flops 536870912 | bytes 8388608 | tf_op jit(solution)/shard_map/expand/pallas_call | solution.py:342
  23.6 2.4 %collective-permute-start = (f32[2,129,8,128]{3,2,1,0:T(8,128)}, f32[2,129,8,128]{3,2,1,0:T(8,128)S(1)}, u32[]{:S(2)}, u32[]{:S(2)}) collective-permute-start(f32[2,129,8,128]{3,2,1,0:T(8,128)} %get-tuple-element.43), channel_id=1, source_target_pairs={{0,16},{1,65},{2,18},{3,67},{4,20},{5,69},{6,22},{7,71},{8,24},{9,... | collective-permute-start | bytes 3170312 | tf_op jit(solution)/shard_map/ppermute | solution.py:586
  26.0 1.4 collective-permute-start.1
  27.4 1.8 %collective-permute-start.2 = (f32[2,129,8,128]{3,2,1,0:T(8,128)}, f32[2,129,8,128]{3,2,1,0:T(8,128)}, u32[]{:S(2)}, u32[]{:S(2)}) collective-permute-start(f32[2,129,8,128]{3,2,1,0:T(8,128)} %get-tuple-element.45), channel_id=1, source_target_pairs={{0,24},{1,97},{2,26},{3,99},{4,28},{5,101},{6,30},{7,103},{8,0},{9... | collective-permute-start | bytes 3170312 | tf_op jit(solution)/shard_map/ppermute | solution.py:586
  29.3 18.4 %expand.3 = (f32[2,129,8,128]{3,2,1,0:T(8,128)}, f32[2,129,8,128]{3,2,1,0:T(8,128)}, f32[2,129,8,128]{3,2,1,0:T(8,128)}, f32[2,129,8,128]{3,2,1,0:T(8,128)}) custom-call(s32[3072]{0:T(1024)} %bitcast.102, f32[16,8,128]{2,1,0:T(8,128)} %get-tuple-element.36.labels, f32[10240,128]{1,0:T(8,128)} %bitcast.100), custom_call_target="tpu_custom_call" | custom-call | flops 536870912 | bytes 8388608 | tf_op jit(solution)/shard_map/expand/pallas_call | solution.py:342
  47.7 1.5 collective-permute-start.3
  49.2 0.6 collective-permute-start.4
  49.8 0.0 collective-permute-done.refs_1_
  49.8 2.6 %collective-permute-start.5 = (f32[2,129,8,128]{3,2,1,0:T(8,128)}, f32[2,129,8,128]{3,2,1,0:T(8,128)}, u32[]{:S(2)}, u32[]{:S(2)}) collective-permute-start(f32[2,129,8,128]{3,2,1,0:T(8,128)} %get-tuple-element.50), channel_id=1, source_target_pairs={{0,24},{1,97},{2,26},{3,99},{4,28},{5,101},{6,30},{7,103},{8,0},{9... | collective-permute-start | bytes 3170312 | tf_op jit(solution)/shard_map/ppermute | solution.py:586
  52.4 0.0 collective-permute-done.1.refs_2_
  52.4 7.9 %gather.2 = (f32[257,8,128]{2,1,0:T(8,128)}, f32[257,8,128]{2,1,0:T(8,128)}) custom-call(f32[2,129,8,128]{3,2,1,0:T(8,128)} %get-tuple-element.42.refs_0_, f32[2,129,8,128]{3,2,1,0:T(8,128)} %copy-done.2, f32[2,129,8,128]{3,2,1,0:T(8,128)} %collective-permute-done.1.refs_2_, f32[2,129,8,128]{3,2,1,0:T(8,128)} %collective-permute-done.2.refs_3_), custom_call_target="tpu_custom_call" | custom-call | flops 134217728 | bytes 8388608 | tf_op jit(solution)/shard_map/gather/pallas_call | solution.py:397
  60.4 3.1 %collective-permute-start.7 = (f32[257,8,128]{2,1,0:T(8,128)}, f32[257,8,128]{2,1,0:T(8,128)S(1)}, u32[]{:S(2)}, u32[]{:S(2)}) collective-permute-start(f32[257,8,128]{2,1,0:T(8,128)} %get-tuple-element.46), channel_id=1, source_target_pairs={{0,64},{1,17},{2,66},{3,19},{4,68},{5,21},{6,70},{7,23},{8,72},{9,... | collective-permute-start | bytes 3158024 | tf_op jit(solution)/shard_map/ppermute | solution.py:586
  63.5 2.2 %collective-permute-start.6 = (f32[257,8,128]{2,1,0:T(8,128)}, f32[257,8,128]{2,1,0:T(8,128)}, u32[]{:S(2)}, u32[]{:S(2)}) collective-permute-start(f32[257,8,128]{2,1,0:T(8,128)} %get-tuple-element.52), channel_id=1, source_target_pairs={{0,32},{1,9},{2,34},{3,11},{4,36},{5,13},{6,38},{7,15},{8,40},{9,1... | collective-permute-start | bytes 3158024 | tf_op jit(solution)/shard_map/ppermute | solution.py:586
  65.7 31.7 %collective-permute-done.4.refs_2_ = f32[2,129,8,128]{3,2,1,0:T(8,128)S(1)} collective-permute-done((f32[2,129,8,128]{3,2,1,0:T(8,128)}, f32[2,129,8,128]{3,2,1,0:T(8,128)S(1)}, u32[]{:S(2)}, u32[]{:S(2)}) %collective-permute-start.4) | collective-permute-done | bytes 1056800 | tf_op jit(solution)/shard_map/ppermute | solution.py:586
  97.5 1.0 copy-done.1
  98.4 7.4 %gather.3 = (f32[257,8,128]{2,1,0:T(8,128)}, f32[257,8,128]{2,1,0:T(8,128)}) custom-call(f32[2,129,8,128]{3,2,1,0:T(8,128)} %get-tuple-element.47.refs_0_, f32[2,129,8,128]{3,2,1,0:T(8,128)} %copy-done, f32[2,129,8,128]{3,2,1,0:T(8,128)} %copy-done.1, f32[2,129,8,128]{3,2,1,0:T(8,128)} %collective-permute-done.5.refs_3_), custom_call_target="tpu_custom_call" | custom-call | flops 134217728 | bytes 8388608 | tf_op jit(solution)/shard_map/gather/pallas_call | solution.py:397
  105.9 4.2 %collective-permute-start.8 = (f32[257,8,128]{2,1,0:T(8,128)}, f32[257,8,128]{2,1,0:T(8,128)S(1)}, u32[]{:S(2)}, u32[]{:S(2)}) collective-permute-start(f32[257,8,128]{2,1,0:T(8,128)} %get-tuple-element.53), channel_id=1, source_target_pairs={{0,96},{1,25},{2,98},{3,27},{4,100},{5,29},{6,102},{7,31},{8,104},... | collective-permute-start | bytes 3158024 | tf_op jit(solution)/shard_map/ppermute | solution.py:586
  110.1 0.1 multiply_bitcast_fusion.1
  110.1 0.1 mul.298
  110.2 0.1 mul.299
  110.3 0.1 mul.314
  110.4 0.1 mul.315
  110.4 0.1 mul.307
  110.5 0.1 mul.308
  110.6 0.1 fusion.14
  110.7 0.0 copy-start.12
  110.7 0.0 copy-start.13
  110.7 0.0 copy-start.14
  110.8 5.1 %fusion.8 = (f32[128,8,128]{2,1,0:T(8,128)}, f32[128,8,128]{2,1,0:T(8,128)}, f32[128,8,128]{2,1,0:T(8,128)}, f32[128,8,128]{2,1,0:T(8,128)}) fusion(f32[8,128]{1,0:T(8,128)S(1)} %fusion.14, f32[8,8,128]{2,1,0:T(8,128)S(1)} %copy-done.9, f32[128]{0:T(128)S(1)} %mul.315, f32[8,8,128]{2,1,0:T(8,128)S(1)} %copy-done.10, f32[128]{0:T(128)S(1)} %mul.308, ...), kind=kLoop, calls=%fused_computation.11 | loop fusion | flops 1179648 | bytes 2201088 | tf_op jit(solution)/shard_map/mul | solution.py:559
  115.8 1.3 sine_multiply_fusion
  117.1 7.2 %phases.1 = (f32[8,32,8,128]{3,2,1,0:T(8,128)}, f32[8,32,8,128]{3,2,1,0:T(8,128)}, f32[8,32,8,128]{3,2,1,0:T(8,128)}, f32[8,32,8,128]{3,2,1,0:T(8,128)}, s32[16,32]{1,0:T(8,128)}) custom-call(s32[4]{0:T(128)} %pad_add_fusion.here, s32[8,32]{1,0:T(8,128)} %bitcast.105, s32[8,32]{1,0:T(8,128)} %bitcast.106, s32[256]{0:T(256)} %bitcast.103, s32[32]{0:T(128)} %bitcast.109, ...), custom_call_target="tpu_custom_call" | custom-call | tf_op jit(solution)/shard_map/phases/pallas_call | solution.py:649
  124.4 0.4 collective-permute-done.8.a3
  124.8 0.6 copy-done.3
  125.3 0.4 copy-done.4
  125.7 9.7 %levels.1 = (f32[256,8,128]{2,1,0:T(8,128)}, f32[4,36,8,128]{3,2,1,0:T(8,128)}, f32[4,36,8,128]{3,2,1,0:T(8,128)}) custom-call(s32[4]{0:T(128)} %pad_add_fusion.here, s32[16,32]{1,0:T(8,128)} %get-tuple-element.41.goal, f32[257,8,128]{2,1,0:T(8,128)} %get-tuple-element.51.a0, f32[257,8,128]{2,1,0:T(8,128)} %collective-permute-done.6.a1, ...), custom_call_target="tpu_custom_call" | custom-call | tf_op jit(solution)/shard_map/levels/pallas_call | solution.py:663
  135.5 2.2 %collective-permute-done.9.got = f32[4,36,8,128]{3,2,1,0:T(8,128)S(1)} collective-permute-done((f32[4,36,8,128]{3,2,1,0:T(8,128)}, f32[4,36,8,128]{3,2,1,0:T(8,128)S(1)}, u32[]{:S(2)}, u32[]{:S(2)}) %collective-permute-start.9) | collective-permute-done | bytes 589856 | tf_op jit(solution)/shard_map/ppermute | solution.py:677
  137.7 0.8 copy-done.5
  138.5 2.2 %merge.1 = (f32[36,8,128]{2,1,0:T(8,128)}, f32[36,8,128]{2,1,0:T(8,128)}, f32[36,8,128]{2,1,0:T(8,128)}, f32[36,8,128]{2,1,0:T(8,128)}) custom-call(s32[4]{0:T(128)} %pad_add_fusion.here, f32[4,36,8,128]{3,2,1,0:T(8,128)} %get-tuple-element.59.mine, f32[4,36,8,128]{3,2,1,0:T(8,128)} %copy-done.5), custom_call_target="tpu_custom_call" | custom-call | tf_op jit(solution)/shard_map/merge/pallas_call | solution.py:678
  140.7 1.8 %collective-permute-start.10 = (f32[36,8,128]{2,1,0:T(8,128)}, f32[36,8,128]{2,1,0:T(8,128)S(1)}, u32[]{:S(2)}, u32[]{:S(2)}) collective-permute-start(f32[36,8,128]{2,1,0:T(8,128)} %get-tuple-element.62), channel_id=1, source_target_pairs={{0,2},{1,3},{2,4},{3,5},{4,6},{5,7},{6,0},{7,1},{8,10},{9,11},{10,... | collective-permute-start | bytes 442376 | tf_op jit(solution)/shard_map/ppermute | solution.py:591
  142.4 3.6 %collective-permute-start.11 = (f32[36,8,128]{2,1,0:T(8,128)}, f32[36,8,128]{2,1,0:T(8,128)S(1)}, u32[]{:S(2)}, u32[]{:S(2)}) collective-permute-start(f32[36,8,128]{2,1,0:T(8,128)} %get-tuple-element.63), channel_id=1, source_target_pairs={{0,4},{1,5},{2,6},{3,7},{4,0},{5,1},{6,2},{7,3},{8,12},{9,13},{10,... | collective-permute-start | bytes 442376 | tf_op jit(solution)/shard_map/ppermute | solution.py:591
  146.1 1.8 %collective-permute-start.12 = (f32[36,8,128]{2,1,0:T(8,128)}, f32[36,8,128]{2,1,0:T(8,128)S(1)}, u32[]{:S(2)}, u32[]{:S(2)}) collective-permute-start(f32[36,8,128]{2,1,0:T(8,128)} %get-tuple-element.64), channel_id=1, source_target_pairs={{0,6},{1,7},{2,0},{3,1},{4,2},{5,3},{6,4},{7,5},{8,14},{9,15},{10,... | collective-permute-start | bytes 442376 | tf_op jit(solution)/shard_map/ppermute | solution.py:591
  147.9 1.1 collective-permute-done.10.g1
  149.0 4.3 %collective-permute-done.11.g2 = f32[36,8,128]{2,1,0:T(8,128)S(1)} collective-permute-done((f32[36,8,128]{2,1,0:T(8,128)}, f32[36,8,128]{2,1,0:T(8,128)S(1)}, u32[]{:S(2)}, u32[]{:S(2)}) %collective-permute-start.11) | collective-permute-done | bytes 147488 | tf_op jit(solution)/shard_map/ppermute | solution.py:591
  153.3 0.7 copy-done.7
  154.0 0.0 copy-done.8
  154.0 1.9 %close.1 = (f32[32,8,128]{2,1,0:T(8,128)}, f32[4,8,128]{2,1,0:T(8,128)}) custom-call(s32[4]{0:T(128)} %pad_add_fusion.here, s32[256]{0:T(256)} %bitcast.104, s32[32]{0:T(128)} %bitcast.110, f32[36,8,128]{2,1,0:T(8,128)} %get-tuple-element.61.g0, f32[36,8,128]{2,1,0:T(8,128)} %copy-done.6, f32[36,8,128]{2,1,0:T(8,128)} %copy-done.7, f32[36,8,128]{2,1,0:T(8,128)} %copy-done.8, ...), custom_call_target="tpu_custom_call" | custom-call | tf_op jit(solution)/shard_map/close/pallas_call | solution.py:686
  (32 shorter events, 0.1 us)
Async XLA Ops:
  23.6 26.1 %collective-permute-start = (f32[2,129,8,128]{3,2,1,0:T(8,128)}, f32[2,129,8,128]{3,2,1,0:T(8,128)S(1)}, u32[]{:S(2)}, u32[]{:S(2)}) collective-permute-start(f32[2,129,8,128]{3,2,1,0:T(8,128)} %get-tuple-element.43), channel_id=1, source_target_pairs={{0,16},{1,65},{2,18},{3,67},{4,20},{5,69},{6,22},{7,71},{8,24},{9,... | collective-permute-start | bytes 3170312 | tf_op jit(solution)/shard_map/ppermute | solution.py:586
  26.0 26.4 %collective-permute-start.1 = (f32[2,129,8,128]{3,2,1,0:T(8,128)}, f32[2,129,8,128]{3,2,1,0:T(8,128)}, u32[]{:S(2)}, u32[]{:S(2)}) collective-permute-start(f32[2,129,8,128]{3,2,1,0:T(8,128)} %get-tuple-element.44), channel_id=1, source_target_pairs={{0,8},{1,33},{2,10},{3,35},{4,12},{5,37},{6,14},{7,39},{8,16},{9,4... | collective-permute-start | bytes 3170312 | tf_op jit(solution)/shard_map/ppermute | solution.py:586
  27.4 25.0 %collective-permute-start.2 = (f32[2,129,8,128]{3,2,1,0:T(8,128)}, f32[2,129,8,128]{3,2,1,0:T(8,128)}, u32[]{:S(2)}, u32[]{:S(2)}) collective-permute-start(f32[2,129,8,128]{3,2,1,0:T(8,128)} %get-tuple-element.45), channel_id=1, source_target_pairs={{0,24},{1,97},{2,26},{3,99},{4,28},{5,101},{6,30},{7,103},{8,0},{9... | collective-permute-start | bytes 3170312 | tf_op jit(solution)/shard_map/ppermute | solution.py:586
  47.7 18.0 %collective-permute-start.3 = (f32[2,129,8,128]{3,2,1,0:T(8,128)}, f32[2,129,8,128]{3,2,1,0:T(8,128)S(1)}, u32[]{:S(2)}, u32[]{:S(2)}) collective-permute-start(f32[2,129,8,128]{3,2,1,0:T(8,128)} %get-tuple-element.48), channel_id=1, source_target_pairs={{0,16},{1,65},{2,18},{3,67},{4,20},{5,69},{6,22},{7,71},{8,24},{9,... | collective-permute-start | bytes 3170312 | tf_op jit(solution)/shard_map/ppermute | solution.py:586
  49.2 48.3 %collective-permute-start.4 = (f32[2,129,8,128]{3,2,1,0:T(8,128)}, f32[2,129,8,128]{3,2,1,0:T(8,128)S(1)}, u32[]{:S(2)}, u32[]{:S(2)}) collective-permute-start(f32[2,129,8,128]{3,2,1,0:T(8,128)} %get-tuple-element.49), channel_id=1, source_target_pairs={{0,8},{1,33},{2,10},{3,35},{4,12},{5,37},{6,14},{7,39},{8,16},{9,4... | collective-permute-start | bytes 3170312 | tf_op jit(solution)/shard_map/ppermute | solution.py:586
  49.8 2.6 %copy-start.2 = (f32[2,129,8,128]{3,2,1,0:T(8,128)}, f32[2,129,8,128]{3,2,1,0:T(8,128)S(1)}, u32[]{:S(2)}) copy-start(f32[2,129,8,128]{3,2,1,0:T(8,128)S(1)} %collective-permute-done.refs_1_) | copy-start | bytes 3170308
  49.8 47.7 %collective-permute-start.5 = (f32[2,129,8,128]{3,2,1,0:T(8,128)}, f32[2,129,8,128]{3,2,1,0:T(8,128)}, u32[]{:S(2)}, u32[]{:S(2)}) collective-permute-start(f32[2,129,8,128]{3,2,1,0:T(8,128)} %get-tuple-element.50), channel_id=1, source_target_pairs={{0,24},{1,97},{2,26},{3,99},{4,28},{5,101},{6,30},{7,103},{8,0},{9... | collective-permute-start | bytes 3170312 | tf_op jit(solution)/shard_map/ppermute | solution.py:586
  60.4 64.0 %collective-permute-start.7 = (f32[257,8,128]{2,1,0:T(8,128)}, f32[257,8,128]{2,1,0:T(8,128)S(1)}, u32[]{:S(2)}, u32[]{:S(2)}) collective-permute-start(f32[257,8,128]{2,1,0:T(8,128)} %get-tuple-element.46), channel_id=1, source_target_pairs={{0,64},{1,17},{2,66},{3,19},{4,68},{5,21},{6,70},{7,23},{8,72},{9,... | collective-permute-start | bytes 3158024 | tf_op jit(solution)/shard_map/ppermute | solution.py:586
  63.5 46.6 %copy-start.15 = (f32[16,2]{0,1:T(2,128)S(1)}, f32[16,2]{0,1:T(2,128)}, u32[]{:S(2)}) copy-start(f32[16,2]{0,1:T(2,128)} %param.21) | copy-start | bytes 388
  63.5 47.3 %copy-start.9 = (f32[8,8,128]{2,1,0:T(8,128)S(1)}, f32[8,8,128]{2,1,0:T(8,128)}, u32[]{:S(2)}) copy-start(f32[8,8,128]{2,1,0:T(8,128)} %constant.103) | copy-start | bytes 98308
  63.5 47.3 %copy-start.10 = (f32[8,8,128]{2,1,0:T(8,128)S(1)}, f32[8,8,128]{2,1,0:T(8,128)}, u32[]{:S(2)}) copy-start(f32[8,8,128]{2,1,0:T(8,128)} %constant.101) | copy-start | bytes 98308
  63.5 47.3 %copy-start.11 = (f32[8,8,128]{2,1,0:T(8,128)S(1)}, f32[8,8,128]{2,1,0:T(8,128)}, u32[]{:S(2)}) copy-start(f32[8,8,128]{2,1,0:T(8,128)} %constant.99) | copy-start | bytes 98308
  63.5 60.9 %collective-permute-start.6 = (f32[257,8,128]{2,1,0:T(8,128)}, f32[257,8,128]{2,1,0:T(8,128)}, u32[]{:S(2)}, u32[]{:S(2)}) collective-permute-start(f32[257,8,128]{2,1,0:T(8,128)} %get-tuple-element.52), channel_id=1, source_target_pairs={{0,32},{1,9},{2,34},{3,11},{4,36},{5,13},{6,38},{7,15},{8,40},{9,1... | collective-permute-start | bytes 3158024 | tf_op jit(solution)/shard_map/ppermute | solution.py:586
  65.7 31.8 %copy-start = (f32[2,129,8,128]{3,2,1,0:T(8,128)}, f32[2,129,8,128]{3,2,1,0:T(8,128)S(1)}, u32[]{:S(2)}) copy-start(f32[2,129,8,128]{3,2,1,0:T(8,128)S(1)} %collective-permute-done.3.refs_1_) | copy-start | bytes 3170308
  97.4 1.0 copy-start.1
  105.9 18.9 %collective-permute-start.8 = (f32[257,8,128]{2,1,0:T(8,128)}, f32[257,8,128]{2,1,0:T(8,128)S(1)}, u32[]{:S(2)}, u32[]{:S(2)}) collective-permute-start(f32[257,8,128]{2,1,0:T(8,128)} %get-tuple-element.53), channel_id=1, source_target_pairs={{0,96},{1,25},{2,98},{3,27},{4,100},{5,29},{6,102},{7,31},{8,104},... | collective-permute-start | bytes 3158024 | tf_op jit(solution)/shard_map/ppermute | solution.py:586
  110.7 5.1 %copy-start.12 = (f32[8,128]{1,0:T(8,128)S(1)}, f32[8,128]{1,0:T(8,128)}, u32[]{:S(2)}) copy-start(f32[8,128]{1,0:T(8,128)} %constant.109) | copy-start | bytes 12292
  110.7 5.1 %copy-start.13 = (f32[8,128]{1,0:T(8,128)S(1)}, f32[8,128]{1,0:T(8,128)}, u32[]{:S(2)}) copy-start(f32[8,128]{1,0:T(8,128)} %constant.107) | copy-start | bytes 12292
  110.7 5.1 %copy-start.14 = (f32[8,128]{1,0:T(8,128)S(1)}, f32[8,128]{1,0:T(8,128)}, u32[]{:S(2)}) copy-start(f32[8,128]{1,0:T(8,128)} %constant.105) | copy-start | bytes 12292
  124.3 1.0 copy-start.3
  124.7 1.0 copy-start.4
  135.5 2.2 %collective-permute-start.9 = (f32[4,36,8,128]{3,2,1,0:T(8,128)}, f32[4,36,8,128]{3,2,1,0:T(8,128)S(1)}, u32[]{:S(2)}, u32[]{:S(2)}) collective-permute-start(f32[4,36,8,128]{3,2,1,0:T(8,128)} %get-tuple-element.60), channel_id=1, source_target_pairs={{0,1},{1,0},{2,3},{3,2},{4,5},{5,4},{6,7},{7,6},{8,9},{9,8},{10,11... | collective-permute-start | bytes 1769480 | tf_op jit(solution)/shard_map/ppermute | solution.py:677
  137.7 0.8 copy-start.5
  140.7 8.3 %collective-permute-start.10 = (f32[36,8,128]{2,1,0:T(8,128)}, f32[36,8,128]{2,1,0:T(8,128)S(1)}, u32[]{:S(2)}, u32[]{:S(2)}) collective-permute-start(f32[36,8,128]{2,1,0:T(8,128)} %get-tuple-element.62), channel_id=1, source_target_pairs={{0,2},{1,3},{2,4},{3,5},{4,6},{5,7},{6,0},{7,1},{8,10},{9,11},{10,... | collective-permute-start | bytes 442376 | tf_op jit(solution)/shard_map/ppermute | solution.py:591
  142.4 10.9 %collective-permute-start.11 = (f32[36,8,128]{2,1,0:T(8,128)}, f32[36,8,128]{2,1,0:T(8,128)S(1)}, u32[]{:S(2)}, u32[]{:S(2)}) collective-permute-start(f32[36,8,128]{2,1,0:T(8,128)} %get-tuple-element.63), channel_id=1, source_target_pairs={{0,4},{1,5},{2,6},{3,7},{4,0},{5,1},{6,2},{7,3},{8,12},{9,13},{10,... | collective-permute-start | bytes 442376 | tf_op jit(solution)/shard_map/ppermute | solution.py:591
  146.1 7.2 %collective-permute-start.12 = (f32[36,8,128]{2,1,0:T(8,128)}, f32[36,8,128]{2,1,0:T(8,128)S(1)}, u32[]{:S(2)}, u32[]{:S(2)}) collective-permute-start(f32[36,8,128]{2,1,0:T(8,128)} %get-tuple-element.64), channel_id=1, source_target_pairs={{0,6},{1,7},{2,0},{3,1},{4,2},{5,3},{6,4},{7,5},{8,14},{9,15},{10,... | collective-permute-start | bytes 442376 | tf_op jit(solution)/shard_map/ppermute | solution.py:591
  149.0 4.3 %copy-start.6 = (f32[36,8,128]{2,1,0:T(8,128)}, f32[36,8,128]{2,1,0:T(8,128)S(1)}, u32[]{:S(2)}) copy-start(f32[36,8,128]{2,1,0:T(8,128)S(1)} %collective-permute-done.10.g1) | copy-start | bytes 442372
  153.3 0.7 copy-start.7
  153.3 0.7 copy-start.8
where the time goes:
time: 156 us
  Pallas kernels  77.1 us (49%)
  waiting for transfers between devices  39.8 us (26%)
  starting transfers between devices  27.1 us (17%)
  other arithmetic  7.1 us (5%)
  local copies, waits for them, and re-layouts  4.02 us (3%)
    pallas_call x2, Pallas kernels, expand(): pl.pallas_call(functools.partial(expand_kernel, chunk), out_shape=[jax.Sh...  38.1 us
    ppermute x9, waiting for transfers between devices, hop(): return lax.ppermute(x, ('sfc', 'grp'), pairs)  32.2 us
    ppermute x9, starting transfers between devices, hop(): return lax.ppermute(x, ('sfc', 'grp'), pairs)  19.9 us
    pallas_call x2, Pallas kernels, gather(): pl.pallas_call(functools.partial(gather_kernel, wide), out_shape=[jax.Sha...  15.3 us
    pallas_call x1, Pallas kernels, per_device(): pl.pallas_call(levels_kernel, out_shape=(tiles(leaf_count), tiles(4, SEAT...  9.75 us
    ppermute x3, starting transfers between devices, around(): return lax.ppermute(x, 'grp', pairs)  7.23 us
    pallas_call x1, Pallas kernels, per_device(): make_phases(here, leaf_slots[0], box_slots[0], parent_cone[0], box_cone[0...  7.19 us
    mul x2, other arithmetic, phase_tables(): return (jnp.cos(angle), jnp.sin(angle) * sign)  6.35 us
  transfers between devices with their start and end apart: 13, of which 5 were waited for; matrix products, arithmetic and copies ran while one was open for 4% of the time, Pallas kernels for 26%

commit v1 on v0

--- a/solution.py
+++ b/solution.py
@@ -9,7 +9,6 @@
 from jax.sharding import PartitionSpec as P
 
 kappa_leaf = 2.0
-kappa_box = 4.0
 f32 = jnp.float32
 i32 = jnp.int32
 VMEM = pl.BlockSpec(memory_space=pltpu.VMEM)
@@ -39,15 +38,6 @@
 
 def axis_maps():
     return np.stack([lagrange_np(child_axis(bit)) for bit in range(2)])
-
-
-def tile_of_nodes(first, second, third):
-    rows = np.arange(8)[:, None]
-    lanes = np.arange(128)[None, :]
-    a = 2 * (rows // 2) + lanes // 64
-    b = lanes % 64 // 8 + 0 * rows
-    c = lanes % 8 + 0 * rows
-    return np.stack([first[a], second[b], third[c]])
 
 
 def lane_maps():
@@ -102,7 +92,7 @@
     return lax.broadcasted_iota(i32, shape, len(shape) - 1)
 
 
-CHUNKS = ((2, 1), (3, 0))
+CHUNKS = ((2,), (1, 3), (0,))
 ORDER = tuple(m for chunk in CHUNKS for m in chunk)
 
 
@@ -443,33 +433,68 @@
 SEATS = 36
 
 
+def turn(ca, sa, cb, sb):
+    return ca * cb - sa * sb, sa * cb + ca * sb
+
+
+def twice(c, s):
+    return c * c - s * s, 2.0 * (s * c)
+
+
 def phases_kernel(
-    here, slots, boxes, cones, box_cones, e0c, e0s, e1c, e1s, e2c, e2s, p0c, p0s, p1c, p1s, goal
+    here, slots, boxes, cones, box_cones, cosine, sine, p0c, p0s, p1c, p1s, ec, es, goal,
+    t0c, t0s, t1c, t1s, t2c, t2s,
 ):
     side = here[2]
-    for o in range(8):
-
-        def child(j, carry):
-            p = slots[o, j]
+    sign = jnp.where(rows_of((8, 128)) % 2 == 0, -1.0, 1.0)
+
+    def cone_tables(n, carry):
+        xs = [(cosine[n, v], sine[n, v]) for v in range(3)]
+        wide = [
+            tuple(jnp.broadcast_to(t[n, 3, pl.ds(v, 1), :], (8, 128)) for t in (cosine, sine))
+            for v in range(5)
+        ]
+        t1c[n], t1s[n] = turn(*xs[2], *wide[4])
+        xs2 = [twice(*x) for x in xs[:2]]
+        for v in range(4):
+            wide2 = twice(*wide[v])
+            for bit in range(2):
+                at = n * 8 + 4 * bit + v
+                t0c[at], t0s[at] = turn(*xs[bit], *wide[v])
+                t2c[at], t2s[at] = turn(*xs2[bit], *wide2)
+        return carry
+
+    lax.fori_loop(0, cosine.shape[0], cone_tables, 0)
+
+    def child(j, carry):
+        for o in range(8):
+            p = slots[32 * o + j]
             e = cones[p] * 8 + o
-            p0c[o, j] = e0c[e]
-            p0s[o, j] = e0s[e]
+            p0c[o, j] = t0c[e]
+            p0s[o, j] = t0s[e] * sign
             owner = p >> 5
-            goal[o, j] = ((((owner & 1) ^ side) << 2) + (owner >> 1)) * SEATS + (p & 31)
-            q = boxes[o, j]
+            goal[32 * o + j] = ((((owner & 1) ^ side) << 2) + (owner >> 1)) * SEATS + (p & 31)
             a = cones[8 * j + o]
-            b = box_cones[q] * 8 + o
-            ca, sa, cb, sb = e1c[a], e1s[a], e2c[b], e2s[b]
-            p1c[o, j] = ca * cb - sa * sb
-            p1s[o, j] = sa * cb + ca * sb
-            owner = q >> 2
-            goal[8 + o, j] = ((((owner & 1) ^ side) << 2) + (owner >> 1)) * SEATS + 32 + (q & 3)
-            return carry
-
-        lax.fori_loop(0, 32, child, 0, unroll=4)
-
-
-def translate(t, both, rows, octant):
+            b = box_cones[boxes[32 * o + j]] * 8 + o
+            c, s = turn(t1c[a], t1s[a], t2c[b], t2s[b])
+            p1c[o, j] = c
+            p1s[o, j] = s * sign
+        return carry
+
+    lax.fori_loop(0, 32, child, 0)
+    me = 2 * here[3] + side
+    for n in range(SEATS):
+        if n < 32:
+            a = cones[32 * me + n]
+            c, s = t1c[a], t1s[a]
+        else:
+            a = box_cones[4 * me + n - 32]
+            c, s = twice(t1c[a], t1s[a])
+        ec[n] = c
+        es[n] = s * sign
+
+
+def lane_mix(t, both, octant):
     count = t.shape[0]
     flat = t.reshape(count * 8, 128)
     high = flat.astype(jnp.bfloat16)
@@ -477,13 +502,15 @@
     res = jnp.dot(
         jnp.concatenate([high, low], axis=1), both[octant % 4], preferred_element_type=f32
     )
-    return row_mix((res[:, :128] + res[:, 128:]).reshape(count, 8, 128), rows, octant // 4)
+    return (res[:, :128] + res[:, 128:]).reshape(count, 8, 128)
 
 
 def levels_kernel(
-    here, goal, a0, a1, a2, a3, p0c, p0s, p1c, p1s, both, rows, leaves, mine, other, acc, moved
+    here, goal, boxes, a0, a1, a2, a3, p0c, p0s, p1c, p1s, both, rows, leaves, mine, other,
+    acc, upper, moved,
 ):
     acc[...] = jnp.zeros(acc.shape, f32)
+    upper[...] = jnp.zeros(upper.shape, f32)
     step = 16
     shape = (step, 8, 128)
     own = rows_of(shape) % 2 == lanes_of(shape) // 64
@@ -498,19 +525,18 @@
 
     lax.fori_loop(0, leaves.shape[0] // step, settle, 0)
 
-    def spread(o, lead):
-        for start in range(0, 32, 8):
-            spots = [goal[lead + o, start + j] for j in range(8)]
-            sums = [acc[spots[j]] + moved[o % 2, start + j] for j in range(8)]
-            for j in range(8):
-                acc[spots[j]] = sums[j]
+    def spread(o, start, ref, spots):
+        sums = [ref[spots[j]] + moved[o % 2, start + j] for j in range(8)]
+        for j in range(8):
+            ref[spots[j]] = sums[j]
 
     for o in range(8):
         for part in range(0, 32, 8):
             t = jnp.stack([leaves[8 * (part + j) + o] for j in range(8)])
             t = spin(t, p0c[o, part : part + 8], p0s[o, part : part + 8])
-            moved[o % 2, part : part + 8] = translate(t, both, rows, o)
-        spread(o, 0)
+            moved[o % 2, part : part + 8] = row_mix(lane_mix(t, both, o), rows, o // 4)
+        for part in range(0, 32, 8):
+            spread(o, part, acc, [goal[32 * o + part + j] for j in range(8)])
 
     apart = [here[2] * 4 * SEATS, (1 - here[2]) * 4 * SEATS]
     for o in range(8):
@@ -521,42 +547,46 @@
                 owner = p // 32
                 tiles.append(acc[(owner // 2) * SEATS + p % 32 + apart[owner % 2]])
             t = spin(jnp.stack(tiles), p1c[o, part : part + 8], p1s[o, part : part + 8])
-            moved[o % 2, part : part + 8] = translate(t, both, rows, o)
-        spread(o, 8)
-    for z in range(4):
-        mine[z] = acc[pl.ds(z * SEATS, SEATS)]
-        other[z] = acc[pl.ds((4 + z) * SEATS, SEATS)]
-
-
-def merge_kernel(here, mine, got, *outs):
+            moved[o % 2, part : part + 8] = lane_mix(t, both, o)
+        for part in range(0, 32, 8):
+            spread(
+                o, part, upper,
+                [boxes[32 * o + part + j] + 32 * (o // 4) for j in range(8)],
+            )
+    for part in range(0, 32, 8):
+        t = row_mix(upper[part : part + 8], rows, 0) + row_mix(upper[32 + part : 40 + part], rows, 1)
+        for j in range(8):
+            q = part + j
+            owner = q // 4
+            acc[(owner // 2) * SEATS + 32 + q % 4 + apart[owner % 2]] = t[j]
     for k in range(4):
         z = (here[3] + k) % 4
-        outs[k][...] = mine[z] + got[z]
-
-
-def close_kernel(here, cones, box_cones, g0, g1, g2, g3, e1c, e1s, e3c, e3s, out_one, out_two):
-    owned, upper = out_one.shape[0], out_two.shape[0]
-    me = 2 * here[3] + here[2]
+        mine[k] = acc[pl.ds(z * SEATS, SEATS)]
+        other[k] = acc[pl.ds((4 + z) * SEATS, SEATS)]
+
+
+def close_kernel(g0, g1, g2, g3, ec, es, out_one, out_two):
+    owned = out_one.shape[0]
     for n in range(SEATS):
-        t = (g0[n] + g1[n]) + (g2[n] + g3[n])
+        t = spin((g0[n] + g1[n]) + (g2[n] + g3[n]), ec[n], es[n])
         if n < owned:
-            e = cones[me * owned + n]
-            out_one[n] = spin(t, e1c[e], e1s[e])
+            out_one[n] = t
         else:
-            e = box_cones[me * upper + n - owned]
-            out_two[n - owned] = spin(t, e3c[e], e3s[e])
-
-
-def phase_tables(directions, kappa, places):
-    grid = jnp.asarray(places.astype(np.float32))
-    angle = (
-        directions[:, 0, None, None, None] * grid[None, :, 0]
-        + directions[:, 1, None, None, None] * grid[None, :, 1]
-        + directions[:, 2, None, None, None] * grid[None, :, 2]
-    )
-    angle = (kappa * angle).reshape(-1, 8, 128)
-    sign = jnp.where(lax.broadcasted_iota(i32, (1, 8, 128), 1) % 2 == 0, -1.0, 1.0).astype(f32)
-    return jnp.cos(angle), jnp.sin(angle) * sign
+            out_two[n - owned] = t
+
+
+def cone_places():
+    nodes = cheb_nodes()
+    rows = np.arange(8)[:, None]
+    lanes = np.arange(128)[None, :]
+    a = 2 * (rows // 2) + lanes // 64
+    out = np.zeros((3, 4, 8, 128))
+    out[0, 0], out[0, 1], out[0, 2] = child_axis(0)[a], child_axis(1)[a], -nodes[a]
+    b, c = np.arange(128) % 64 // 8, np.arange(128) % 8
+    for v in range(4):
+        out[1, 3, v], out[2, 3, v] = child_axis(v // 2)[b], child_axis(v % 2)[c]
+    out[1, 3, 4], out[2, 3, 4] = -nodes[b], -nodes[c]
+    return out.astype(np.float32)
 
 
 def to_nodes(tiles):
@@ -627,28 +657,23 @@
 
     cone_angles = after(cone_angles, sent[0])
     directions = cone_vectors(cone_angles)
-    child = np.stack(
-        [
-            tile_of_nodes(child_axis(o // 4), child_axis(o // 2 % 2), child_axis(o % 2))
-            for o in range(8)
-        ]
-    )
-    nodes = cheb_nodes()
-    parent = tile_of_nodes(nodes, nodes, nodes)[None]
-    e0c, e0s = phase_tables(directions, kappa_leaf, child)
-    e1c, e1s = phase_tables(directions, -kappa_leaf, parent)
-    e2c, e2s = phase_tables(directions, kappa_box, child)
-    e3c, e3s = phase_tables(directions, -kappa_box, parent)
+    places = jnp.asarray(cone_places())
+    angle = (
+        directions[:, 0, None, None, None] * places[None, 0]
+        + directions[:, 1, None, None, None] * places[None, 1]
+        + directions[:, 2, None, None, None] * places[None, 2]
+    ) * kappa_leaf
     make_phases = pl.pallas_call(
         phases_kernel,
-        out_shape=(tiles(8, 32),) * 4 + (jax.ShapeDtypeStruct((16, 32), i32),),
-        in_specs=[SMEM] * 5 + [VMEM] * 6,
-        out_specs=(VMEM,) * 4 + (SMEM,),
+        out_shape=(tiles(8, 32),) * 4 + (tiles(SEATS),) * 2 + (jax.ShapeDtypeStruct((256,), i32),),
+        in_specs=[SMEM] * 5 + [VMEM] * 2,
+        out_specs=(VMEM,) * 6 + (SMEM,),
+        scratch_shapes=[pltpu.VMEM((n, 8, 128), f32) for n in (128, 128, 16, 16, 128, 128)],
         name="phases",
     )
-    p0c, p0s, p1c, p1s, goal = make_phases(
-        here, leaf_slots[0], box_slots[0], parent_cone[0], box_cone[0],
-        e0c, e0s, e1c, e1s, e2c, e2s,
+    slots, boxes = leaf_slots.reshape(-1), box_slots.reshape(-1)
+    p0c, p0s, p1c, p1s, ec, es, goal = make_phases(
+        here, slots, boxes, parent_cone[0], box_cone[0], jnp.cos(angle), jnp.sin(angle)
     )
 
     held = [None] * 4
@@ -663,33 +688,28 @@
     leaves, mine, other = pl.pallas_call(
         levels_kernel,
         out_shape=(tiles(leaf_count), tiles(4, SEATS), tiles(4, SEATS)),
-        in_specs=[SMEM] * 2 + [VMEM] * 10,
+        in_specs=[SMEM] * 3 + [VMEM] * 10,
         out_specs=(VMEM,) * 3,
         scratch_shapes=[
             pltpu.VMEM((8 * SEATS, 8, 128), f32),
+            pltpu.VMEM((64, 8, 128), f32),
             pltpu.VMEM((2, 32, 8, 128), f32),
         ],
         name="levels",
     )(
-        here, goal, *held, p0c, p0s, p1c, p1s,
+        here, goal, boxes, *held, p0c, p0s, p1c, p1s,
         jnp.asarray(lane_maps()), jnp.asarray(row_maps()),
     )
     swapped = lax.ppermute(other, "grp", [(g, g ^ 1) for g in range(groups)])
-    blocks = pl.pallas_call(
-        merge_kernel,
-        out_shape=(tiles(SEATS),) * 4,
-        in_specs=[SMEM] + [VMEM] * 2,
-        out_specs=(VMEM,) * 4,
-        name="merge",
-    )(here, mine, swapped)
+    blocks = [mine[k] + swapped[k] for k in range(4)]
     got = [blocks[0]] + [around(blocks[k], k, groups) for k in (1, 2, 3)]
     one, two = pl.pallas_call(
         close_kernel,
         out_shape=(tiles(first_owned), tiles(second_owned)),
-        in_specs=[SMEM] * 3 + [VMEM] * 8,
+        in_specs=[VMEM] * 6,
         out_specs=(VMEM, VMEM),
         name="close",
-    )(here, parent_cone[0], box_cone[0], *got, e1c, e1s, e3c, e3s)
+    )(*got, ec, es)
     return (to_nodes(leaves), to_nodes(one), to_nodes(two))
 
 

time: 156 us -> 148 us (0.949)
  waiting for transfers between devices: 39.8 us -> 31.5 us
  other arithmetic: 7.1 us -> 4.39 us
  local copies, waits for them, and re-layouts: 4.02 us -> 6.34 us
    ppermute x9 -> x12, waiting for transfers between devices: 32.2 us -> 20.8 us  [hop(): return lax.ppermute(x, ('sfc', 'grp'), pairs)]
    mul x2 -> x0, other arithmetic: 6.35 us -> none  [phase_tables(): return (jnp.cos(angle), jnp.sin(angle) * sign)]
    pallas_call x2 -> x3, Pallas kernels: 38.1 us -> 42.7 us  [expand(): pl.pallas_call(functools.partial(expand_kernel, chunk), out_shape=[jax.Sh...]
    pallas_call x2 -> x1, Pallas kernels: 9.35 us -> 5.73 us  [per_device(): make_phases(here, slots, boxes, parent_cone[0], box_cone[0], jnp.cos(angl...]
    ppermute x3, waiting for transfers between devices: 5.41 us -> 8.48 us  [around(): return lax.ppermute(x, 'grp', pairs)]
    sin x0 -> x1, other arithmetic: none -> 1.91 us  [per_device(): jnp.sin(angle)]
    add x0 -> x1, other arithmetic: none -> 1.83 us  [per_device(): blocks = [mine[k] + swapped[k] for k in range(4)]]
    pallas_call x2 -> x3, Pallas kernels: 15.3 us -> 16.2 us  [gather(): pl.pallas_call(functools.partial(gather_kernel, wide), out_shape=[jax.Sha...]
  transfers between devices with their start and end apart: 13 -> 16, of which waited for: 5 -> 7; matrix products, arithmetic and copies ran while one was open for 4% -> 2% of each run, Pallas kernels for 26% -> 37%
where the time goes in v1:
time: 148 us; the launch traced here: 147 us
  Pallas kernels  78 us (53%)
  waiting for transfers between devices  31.5 us (21%)
  starting transfers between devices  25.9 us (18%)
  local copies, waits for them, and re-layouts  6.34 us (4%)
  other arithmetic  4.39 us (3%)
    pallas_call x3, Pallas kernels, expand(): pl.pallas_call(functools.partial(expand_kernel, chunk), out_shape=[jax.Sh...  42.7 us
    ppermute x12, waiting for transfers between devices, hop(): return lax.ppermute(x, ('sfc', 'grp'), pairs)  20.8 us
    ppermute x12, starting transfers between devices, hop(): return lax.ppermute(x, ('sfc', 'grp'), pairs)  20 us
    pallas_call x3, Pallas kernels, gather(): pl.pallas_call(functools.partial(gather_kernel, wide), out_shape=[jax.Sha...  16.2 us
    pallas_call x1, Pallas kernels, per_device(): pl.pallas_call(levels_kernel, out_shape=(tiles(leaf_count), tiles(4, SEAT...  8.71 us
    ppermute x3, waiting for transfers between devices, around(): return lax.ppermute(x, 'grp', pairs)  8.48 us
    ppermute x3, starting transfers between devices, around(): return lax.ppermute(x, 'grp', pairs)  5.9 us
    pallas_call x1, Pallas kernels, per_device(): make_phases(here, slots, boxes, parent_cone[0], box_cone[0], jnp.cos(angl...  5.73 us
  transfers between devices with their start and end apart: 16, of which 7 were waited for; matrix products, arithmetic and copies ran while one was open for 2% of the time, Pallas kernels for 37%

profile of v1, /device:TPU:0, one launch (start us, length us, event | category | flops | bytes accessed | tf_op | source)
XLA Modules:
  0.0 147.0 jit_solution(2249728403610394049)
XLA Ops:
  0.7 0.6 pad_add_fusion.here
  1.3 2.7 %route.1 = (s32[24,128]{1,0:T(8,128)}, f32[16,8,128]{2,1,0:T(8,128)}) custom-call(s32[4]{0:T(128)} %pad_add_fusion.here, s32[8,128]{1,0:T(8,128)} %bitcast.49, s32[8,128]{1,0:T(8,128)} %bitcast.50), custom_call_target="tpu_custom_call" | custom-call | tf_op jit(solution)/shard_map/route/pallas_call | solution.py:204
  3.9 9.9 %expand.3 = (f32[1,129,8,128]{3,2,1,0:T(8,128)}, f32[1,129,8,128]{3,2,1,0:T(8,128)}, f32[1,129,8,128]{3,2,1,0:T(8,128)}, f32[1,129,8,128]{3,2,1,0:T(8,128)}) custom-call(s32[3072]{0:T(1024)} %bitcast.46, f32[16,8,128]{2,1,0:T(8,128)} %get-tuple-element.38.labels, f32[10240,128]{1,0:T(8,128)} %bitcast.43), custom_call_target="tpu_custom_call" | custom-call | flops 268435456 | bytes 8388608 | tf_op jit(solution)/shard_map/expand/pallas_call | solution.py:332
  13.8 2.8 %collective-permute-start = (f32[1,129,8,128]{3,2,1,0:T(8,128)}, f32[1,129,8,128]{3,2,1,0:T(8,128)}, u32[]{:S(2)}, u32[]{:S(2)}) collective-permute-start(f32[1,129,8,128]{3,2,1,0:T(8,128)} %get-tuple-element.47), channel_id=1, source_target_pairs={{0,16},{1,65},{2,18},{3,67},{4,20},{5,69},{6,22},{7,71},{8,24},{9,... | collective-permute-start | bytes 1585160 | tf_op jit(solution)/shard_map/ppermute | solution.py:616
  16.6 21.8 %expand.4 = (f32[2,129,8,128]{3,2,1,0:T(8,128)}, f32[2,129,8,128]{3,2,1,0:T(8,128)}, f32[2,129,8,128]{3,2,1,0:T(8,128)}, f32[2,129,8,128]{3,2,1,0:T(8,128)}) custom-call(s32[3072]{0:T(1024)} %bitcast.47, f32[16,8,128]{2,1,0:T(8,128)} %get-tuple-element.38.labels, f32[10240,128]{1,0:T(8,128)} %bitcast.44), custom_call_target="tpu_custom_call" | custom-call | flops 536870912 | bytes 8388608 | tf_op jit(solution)/shard_map/expand/pallas_call | solution.py:332
  38.3 0.1 collective-permute-start.3
  38.4 2.8 %collective-permute-start.4 = (f32[2,129,8,128]{3,2,1,0:T(8,128)}, f32[2,129,8,128]{3,2,1,0:T(8,128)S(1)}, u32[]{:S(2)}, u32[]{:S(2)}) collective-permute-start(f32[2,129,8,128]{3,2,1,0:T(8,128)} %get-tuple-element.52), channel_id=1, source_target_pairs={{0,8},{1,33},{2,10},{3,35},{4,12},{5,37},{6,14},{7,39},{8,16},{9,4... | collective-permute-start | bytes 3170312 | tf_op jit(solution)/shard_map/ppermute | solution.py:616
  41.3 0.5 collective-permute-start.5
  41.7 1.5 %collective-permute-start.1 = (f32[1,129,8,128]{3,2,1,0:T(8,128)}, f32[1,129,8,128]{3,2,1,0:T(8,128)}, u32[]{:S(2)}, u32[]{:S(2)}) collective-permute-start(f32[1,129,8,128]{3,2,1,0:T(8,128)} %get-tuple-element.48), channel_id=1, source_target_pairs={{0,8},{1,33},{2,10},{3,35},{4,12},{5,37},{6,14},{7,39},{8,16},{9,4... | collective-permute-start | bytes 1585160 | tf_op jit(solution)/shard_map/ppermute | solution.py:616
  43.3 1.7 %collective-permute-start.2 = (f32[1,129,8,128]{3,2,1,0:T(8,128)}, f32[1,129,8,128]{3,2,1,0:T(8,128)}, u32[]{:S(2)}, u32[]{:S(2)}) collective-permute-start(f32[1,129,8,128]{3,2,1,0:T(8,128)} %get-tuple-element.49), channel_id=1, source_target_pairs={{0,24},{1,97},{2,26},{3,99},{4,28},{5,101},{6,30},{7,103},{8,0},{9... | collective-permute-start | bytes 1585160 | tf_op jit(solution)/shard_map/ppermute | solution.py:616
  45.0 11.1 %expand.5 = (f32[1,129,8,128]{3,2,1,0:T(8,128)}, f32[1,129,8,128]{3,2,1,0:T(8,128)}, f32[1,129,8,128]{3,2,1,0:T(8,128)}, f32[1,129,8,128]{3,2,1,0:T(8,128)}) custom-call(s32[3072]{0:T(1024)} %bitcast.48, f32[16,8,128]{2,1,0:T(8,128)} %get-tuple-element.38.labels, f32[10240,128]{1,0:T(8,128)} %bitcast.45), custom_call_target="tpu_custom_call" | custom-call | flops 268435456 | bytes 8388608 | tf_op jit(solution)/shard_map/expand/pallas_call | solution.py:332
  56.1 15.8 %collective-permute-done.1.refs_2_ = f32[1,129,8,128]{3,2,1,0:T(8,128)} collective-permute-done((f32[1,129,8,128]{3,2,1,0:T(8,128)}, f32[1,129,8,128]{3,2,1,0:T(8,128)}, u32[]{:S(2)}, u32[]{:S(2)}) %collective-permute-start.1) | collective-permute-done | bytes 528416 | tf_op jit(solution)/shard_map/ppermute | solution.py:616
  71.9 0.2 collective-permute-start.6
  72.1 4.4 %gather.3 = f32[257,8,128]{2,1,0:T(8,128)} custom-call(f32[1,129,8,128]{3,2,1,0:T(8,128)} %get-tuple-element.46.refs_0_, f32[1,129,8,128]{3,2,1,0:T(8,128)} %collective-permute-done.refs_1_, f32[1,129,8,128]{3,2,1,0:T(8,128)} %collective-permute-done.1.refs_2_, f32[1,129,8,128]{3,2,1,0:T(8,128)} %collective-permute-done.2.refs_3_), custom_call_target="tpu_custom_call" | custom-call | flops 67108864 | bytes 4194304 | tf_op jit(solution)/shard_map/gather/pallas_call | solution.py:387
  76.6 0.0 copy-start.10
  76.6 0.0 copy-start.11
  76.6 0.0 copy-start.12
  76.7 5.1 %collective-permute-start.10 = (f32[257,8,128]{2,1,0:T(8,128)}, f32[257,8,128]{2,1,0:T(8,128)}, u32[]{:S(2)}, u32[]{:S(2)}) collective-permute-start(f32[257,8,128]{2,1,0:T(8,128)} %gather.3), channel_id=1, source_target_pairs={{0,64},{1,17},{2,66},{3,19},{4,68},{5,21},{6,70},{7,23},{8,72},{9,... | collective-permute-start | bytes 3158024 | tf_op jit(solution)/shard_map/ppermute | solution.py:616
  81.7 1.0 copy-done
  82.8 0.3 copy-done.1
  83.1 1.0 copy-done.2
  84.1 7.8 %gather.4 = (f32[257,8,128]{2,1,0:T(8,128)}, f32[257,8,128]{2,1,0:T(8,128)}) custom-call(f32[2,129,8,128]{3,2,1,0:T(8,128)} %get-tuple-element.50.refs_0_, f32[2,129,8,128]{3,2,1,0:T(8,128)} %copy-done, f32[2,129,8,128]{3,2,1,0:T(8,128)} %copy-done.1, f32[2,129,8,128]{3,2,1,0:T(8,128)} %copy-done.2), custom_call_target="tpu_custom_call" | custom-call | flops 134217728 | bytes 8388608 | tf_op jit(solution)/shard_map/gather/pallas_call | solution.py:387
  91.8 0.1 collective-permute-start.11
  91.9 2.0 %collective-permute-start.9 = (f32[257,8,128]{2,1,0:T(8,128)}, f32[257,8,128]{2,1,0:T(8,128)S(1)}, u32[]{:S(2)}, u32[]{:S(2)}) collective-permute-start(f32[257,8,128]{2,1,0:T(8,128)} %get-tuple-element.54), channel_id=1, source_target_pairs={{0,32},{1,9},{2,34},{3,11},{4,36},{5,13},{6,38},{7,15},{8,40},{9,1... | collective-permute-start | bytes 3158024 | tf_op jit(solution)/shard_map/ppermute | solution.py:616
  93.9 2.2 %collective-permute-start.7 = (f32[1,129,8,128]{3,2,1,0:T(8,128)}, f32[1,129,8,128]{3,2,1,0:T(8,128)S(1)}, u32[]{:S(2)}, u32[]{:S(2)}) collective-permute-start(f32[1,129,8,128]{3,2,1,0:T(8,128)} %get-tuple-element.57), channel_id=1, source_target_pairs={{0,8},{1,33},{2,10},{3,35},{4,12},{5,37},{6,14},{7,39},{8,16},{9,4... | collective-permute-start | bytes 1585160 | tf_op jit(solution)/shard_map/ppermute | solution.py:616
  96.1 1.0 collective-permute-start.8
  97.2 0.6 reshape.78.boxes
  97.8 0.6 reshape.77.slots
  98.5 0.1 multiply_bitcast_fusion.1
  98.6 1.9 %fusion = (f32[16,4,8,128]{3,2,1,0:T(8,128)}, f32[16,4,8,128]{3,2,1,0:T(8,128)}) fusion(f32[4,8,128]{2,1,0:T(8,128)S(1)} %copy-done.10, f32[16]{0:T(128)S(1)} %get-tuple-element.78, f32[4,8,128]{2,1,0:T(8,128)S(1)} %copy-done.11, f32[16]{0:T(128)S(1)} %get-tuple-element.79, f32[4,8,128]{2,1,0:T(8,128)S(1)} %copy-done.12, f32[16]{0:T(128)S(1)} %get-tuple-element.77), kind=kLoop, calls=%fused_computation.1 | loop fusion | flops 393216 | bytes 573632 | tf_op jit(solution)/shard_map/sin | solution.py:676
  100.5 5.7 %phases.1 = (f32[8,32,8,128]{3,2,1,0:T(8,128)}, f32[8,32,8,128]{3,2,1,0:T(8,128)}, f32[8,32,8,128]{3,2,1,0:T(8,128)}, f32[8,32,8,128]{3,2,1,0:T(8,128)}, f32[36,...) custom-call(s32[4]{0:T(128)} %pad_add_fusion.here, s32[256]{0:T(256)} %reshape.77.slots, s32[256]{0:T(256)} %reshape.78.boxes, ...), custom_call_target="tpu_custom_call" | custom-call | tf_op jit(solution)/shard_map/phases/pallas_call | solution.py:675
  106.2 4.1 %collective-permute-done.7.refs_2_ = f32[1,129,8,128]{3,2,1,0:T(8,128)S(1)} collective-permute-done((f32[1,129,8,128]{3,2,1,0:T(8,128)}, f32[1,129,8,128]{3,2,1,0:T(8,128)S(1)}, u32[]{:S(2)}, u32[]{:S(2)}) %collective-permute-start.7) | collective-permute-done | bytes 528416 | tf_op jit(solution)/shard_map/ppermute | solution.py:616
  110.3 0.9 collective-permute-done.8.refs_3_
  111.1 0.8 copy-done.6
  111.9 4.0 %gather.5.a0 = f32[257,8,128]{2,1,0:T(8,128)} custom-call(f32[1,129,8,128]{3,2,1,0:T(8,128)} %get-tuple-element.55.refs_0_, f32[1,129,8,128]{3,2,1,0:T(8,128)} %collective-permute-done.6.refs_1_, f32[1,129,8,128]{3,2,1,0:T(8,128)} %copy-done.5, f32[1,129,8,128]{3,2,1,0:T(8,128)} %copy-done.6), custom_call_target="tpu_custom_call" | custom-call | flops 67108864 | bytes 4194304 | tf_op jit(solution)/shard_map/gather/pallas_call | solution.py:387
  116.0 1.0 copy-done.3
  116.9 0.3 copy-done.4
  117.3 8.7 %levels.1 = (f32[256,8,128]{2,1,0:T(8,128)}, f32[4,36,8,128]{3,2,1,0:T(8,128)}, f32[4,36,8,128]{3,2,1,0:T(8,128)}) custom-call(s32[4]{0:T(128)} %pad_add_fusion.here, s32[256]{0:T(256)} %get-tuple-element.45.goal, s32[256]{0:T(256)} %reshape.78.boxes, f32[257,8,128]{2,1,0:T(8,128)} %gather.5.a0, f32[257,8,128]{2,1,0:T(8,128)} %copy-done.4, ...), custom_call_target="tpu_custom_call" | custom-call | tf_op jit(solution)/shard_map/levels/pallas_call | solution.py:688
  126.0 2.2 %collective-permute-done.12 = f32[4,36,8,128]{3,2,1,0:T(8,128)S(1)} collective-permute-done((f32[4,36,8,128]{3,2,1,0:T(8,128)}, f32[4,36,8,128]{3,2,1,0:T(8,128)S(1)}, u32[]{:S(2)}, u32[]{:S(2)}) %collective-permute-start.12) | collective-permute-done | bytes 589856 | tf_op jit(solution)/shard_map/ppermute | solution.py:703
  128.2 1.8 %fusion.2 = (f32[36,8,128]{2,1,0:T(8,128)S(1)}, f32[36,8,128]{2,1,0:T(8,128)S(1)}, f32[36,8,128]{2,1,0:T(8,128)S(1)}, f32[36,8,128]{2,1,0:T(8,128)}) fusion(f32[4,36,8,128]{3,2,1,0:T(8,128)S(1)} %collective-permute-done.12, f32[4,36,8,128]{3,2,1,0:T(8,128)} %get-tuple-element.65), kind=kLoop, calls=%fused_computation.4 | loop fusion | flops 147456 | bytes 1769472 | tf_op jit(solution)/shard_map/add | solution.py:704
  130.0 4.1 %collective-permute-start.15 = (f32[36,8,128]{2,1,0:T(8,128)S(1)}, f32[36,8,128]{2,1,0:T(8,128)S(1)}, u32[]{:S(2)}, u32[]{:S(2)}) collective-permute-start(f32[36,8,128]{2,1,0:T(8,128)S(1)} %get-tuple-element.71), channel_id=1, source_target_pairs={{0,6},{1,7},{2,0},{3,1},{4,2},{5,3},{6,4},{7,5},{8,14},{9,15},{10,... | collective-permute-start | bytes 442376 | tf_op jit(solution)/shard_map/ppermute | solution.py:621
  134.1 0.4 collective-permute-start.14
  134.5 1.4 collective-permute-start.13
  135.9 4.8 %collective-permute-done.15.g3 = f32[36,8,128]{2,1,0:T(8,128)S(1)} collective-permute-done((f32[36,8,128]{2,1,0:T(8,128)S(1)}, f32[36,8,128]{2,1,0:T(8,128)S(1)}, u32[]{:S(2)}, u32[]{:S(2)}) %collective-permute-start.15) | collective-permute-done | bytes 147488 | tf_op jit(solution)/shard_map/ppermute | solution.py:621
  140.7 1.7 %collective-permute-done.14.g2 = f32[36,8,128]{2,1,0:T(8,128)S(1)} collective-permute-done((f32[36,8,128]{2,1,0:T(8,128)S(1)}, f32[36,8,128]{2,1,0:T(8,128)S(1)}, u32[]{:S(2)}, u32[]{:S(2)}) %collective-permute-start.14) | collective-permute-done | bytes 147488 | tf_op jit(solution)/shard_map/ppermute | solution.py:621
  142.4 2.0 %collective-permute-done.13.g1 = f32[36,8,128]{2,1,0:T(8,128)S(1)} collective-permute-done((f32[36,8,128]{2,1,0:T(8,128)S(1)}, f32[36,8,128]{2,1,0:T(8,128)S(1)}, u32[]{:S(2)}, u32[]{:S(2)}) %collective-permute-start.13) | collective-permute-done | bytes 147488 | tf_op jit(solution)/shard_map/ppermute | solution.py:621
  144.4 0.6 copy-done.9
  145.1 1.9 %close.1 = (f32[32,8,128]{2,1,0:T(8,128)}, f32[4,8,128]{2,1,0:T(8,128)}) custom-call(f32[36,8,128]{2,1,0:T(8,128)} %get-tuple-element.74.g0, f32[36,8,128]{2,1,0:T(8,128)} %copy-done.9, f32[36,8,128]{2,1,0:T(8,128)} %copy-done.8, f32[36,8,128]{2,1,0:T(8,128)} %copy-done.7, f32[36,8,128]{2,1,0:T(8,128)} %get-tuple-element.67.ec, ...), custom_call_target="tpu_custom_call" | custom-call | tf_op jit(solution)/shard_map/close/pallas_call | solution.py:706
  (32 shorter events, 0.1 us)
Async XLA Ops:
  13.8 29.5 %collective-permute-start = (f32[1,129,8,128]{3,2,1,0:T(8,128)}, f32[1,129,8,128]{3,2,1,0:T(8,128)}, u32[]{:S(2)}, u32[]{:S(2)}) collective-permute-start(f32[1,129,8,128]{3,2,1,0:T(8,128)} %get-tuple-element.47), channel_id=1, source_target_pairs={{0,16},{1,65},{2,18},{3,67},{4,20},{5,69},{6,22},{7,71},{8,24},{9,... | collective-permute-start | bytes 1585160 | tf_op jit(solution)/shard_map/ppermute | solution.py:616
  38.3 43.4 %collective-permute-start.3 = (f32[2,129,8,128]{3,2,1,0:T(8,128)}, f32[2,129,8,128]{3,2,1,0:T(8,128)S(1)}, u32[]{:S(2)}, u32[]{:S(2)}) collective-permute-start(f32[2,129,8,128]{3,2,1,0:T(8,128)} %get-tuple-element.51), channel_id=1, source_target_pairs={{0,16},{1,65},{2,18},{3,67},{4,20},{5,69},{6,22},{7,71},{8,24},{9,... | collective-permute-start | bytes 3170312 | tf_op jit(solution)/shard_map/ppermute | solution.py:616
  38.4 43.3 %collective-permute-start.4 = (f32[2,129,8,128]{3,2,1,0:T(8,128)}, f32[2,129,8,128]{3,2,1,0:T(8,128)S(1)}, u32[]{:S(2)}, u32[]{:S(2)}) collective-permute-start(f32[2,129,8,128]{3,2,1,0:T(8,128)} %get-tuple-element.52), channel_id=1, source_target_pairs={{0,8},{1,33},{2,10},{3,35},{4,12},{5,37},{6,14},{7,39},{8,16},{9,4... | collective-permute-start | bytes 3170312 | tf_op jit(solution)/shard_map/ppermute | solution.py:616
  41.3 40.5 %collective-permute-start.5 = (f32[2,129,8,128]{3,2,1,0:T(8,128)}, f32[2,129,8,128]{3,2,1,0:T(8,128)S(1)}, u32[]{:S(2)}, u32[]{:S(2)}) collective-permute-start(f32[2,129,8,128]{3,2,1,0:T(8,128)} %get-tuple-element.53), channel_id=1, source_target_pairs={{0,24},{1,97},{2,26},{3,99},{4,28},{5,101},{6,30},{7,103},{8,0},{9... | collective-permute-start | bytes 3170312 | tf_op jit(solution)/shard_map/ppermute | solution.py:616
  41.7 30.2 %collective-permute-start.1 = (f32[1,129,8,128]{3,2,1,0:T(8,128)}, f32[1,129,8,128]{3,2,1,0:T(8,128)}, u32[]{:S(2)}, u32[]{:S(2)}) collective-permute-start(f32[1,129,8,128]{3,2,1,0:T(8,128)} %get-tuple-element.48), channel_id=1, source_target_pairs={{0,8},{1,33},{2,10},{3,35},{4,12},{5,37},{6,14},{7,39},{8,16},{9,4... | collective-permute-start | bytes 1585160 | tf_op jit(solution)/shard_map/ppermute | solution.py:616
  43.3 28.8 %collective-permute-start.2 = (f32[1,129,8,128]{3,2,1,0:T(8,128)}, f32[1,129,8,128]{3,2,1,0:T(8,128)}, u32[]{:S(2)}, u32[]{:S(2)}) collective-permute-start(f32[1,129,8,128]{3,2,1,0:T(8,128)} %get-tuple-element.49), channel_id=1, source_target_pairs={{0,24},{1,97},{2,26},{3,99},{4,28},{5,101},{6,30},{7,103},{8,0},{9... | collective-permute-start | bytes 1585160 | tf_op jit(solution)/shard_map/ppermute | solution.py:616
  71.9 24.2 %collective-permute-start.6 = (f32[1,129,8,128]{3,2,1,0:T(8,128)}, f32[1,129,8,128]{3,2,1,0:T(8,128)}, u32[]{:S(2)}, u32[]{:S(2)}) collective-permute-start(f32[1,129,8,128]{3,2,1,0:T(8,128)} %get-tuple-element.56), channel_id=1, source_target_pairs={{0,16},{1,65},{2,18},{3,67},{4,20},{5,69},{6,22},{7,71},{8,24},{9,... | collective-permute-start | bytes 1585160 | tf_op jit(solution)/shard_map/ppermute | solution.py:616
  76.6 20.6 %copy-start.13 = (s32[1,8,32]{2,1,0:T(8,128)S(1)}, s32[1,8,32]{2,1,0:T(8,128)}, u32[]{:S(2)}) copy-start(s32[1,8,32]{2,1,0:T(8,128)} %param.15) | copy-start | bytes 3076
  76.6 21.2 %copy-start.14 = (s32[1,8,32]{2,1,0:T(8,128)S(1)}, s32[1,8,32]{2,1,0:T(8,128)}, u32[]{:S(2)}) copy-start(s32[1,8,32]{2,1,0:T(8,128)} %param.14) | copy-start | bytes 3076
  76.6 21.9 %copy-start.15 = (f32[16,2]{0,1:T(2,128)S(1)}, f32[16,2]{0,1:T(2,128)}, u32[]{:S(2)}) copy-start(f32[16,2]{0,1:T(2,128)} %param.18) | copy-start | bytes 388
  76.6 21.9 %copy-start.10 = (f32[4,8,128]{2,1,0:T(8,128)S(1)}, f32[4,8,128]{2,1,0:T(8,128)}, u32[]{:S(2)}) copy-start(f32[4,8,128]{2,1,0:T(8,128)} %constant.71) | copy-start | bytes 49156
  76.6 21.9 %copy-start.11 = (f32[4,8,128]{2,1,0:T(8,128)S(1)}, f32[4,8,128]{2,1,0:T(8,128)}, u32[]{:S(2)}) copy-start(f32[4,8,128]{2,1,0:T(8,128)} %constant.69) | copy-start | bytes 49156
  76.6 21.9 %copy-start.12 = (f32[4,8,128]{2,1,0:T(8,128)S(1)}, f32[4,8,128]{2,1,0:T(8,128)}, u32[]{:S(2)}) copy-start(f32[4,8,128]{2,1,0:T(8,128)} %constant.67) | copy-start | bytes 49156
  76.7 39.3 %collective-permute-start.10 = (f32[257,8,128]{2,1,0:T(8,128)}, f32[257,8,128]{2,1,0:T(8,128)}, u32[]{:S(2)}, u32[]{:S(2)}) collective-permute-start(f32[257,8,128]{2,1,0:T(8,128)} %gather.3), channel_id=1, source_target_pairs={{0,64},{1,17},{2,66},{3,19},{4,68},{5,21},{6,70},{7,23},{8,72},{9,... | collective-permute-start | bytes 3158024 | tf_op jit(solution)/shard_map/ppermute | solution.py:616
  81.7 1.1 copy-start
  81.7 1.4 copy-start.1
  83.1 1.0 copy-start.2
  91.8 24.1 %collective-permute-start.11 = (f32[257,8,128]{2,1,0:T(8,128)}, f32[257,8,128]{2,1,0:T(8,128)S(1)}, u32[]{:S(2)}, u32[]{:S(2)}) collective-permute-start(f32[257,8,128]{2,1,0:T(8,128)} %get-tuple-element.59), channel_id=1, source_target_pairs={{0,96},{1,25},{2,98},{3,27},{4,100},{5,29},{6,102},{7,31},{8,104},... | collective-permute-start | bytes 3158024 | tf_op jit(solution)/shard_map/ppermute | solution.py:616
  91.9 24.0 %collective-permute-start.9 = (f32[257,8,128]{2,1,0:T(8,128)}, f32[257,8,128]{2,1,0:T(8,128)S(1)}, u32[]{:S(2)}, u32[]{:S(2)}) collective-permute-start(f32[257,8,128]{2,1,0:T(8,128)} %get-tuple-element.54), channel_id=1, source_target_pairs={{0,32},{1,9},{2,34},{3,11},{4,36},{5,13},{6,38},{7,15},{8,40},{9,1... | collective-permute-start | bytes 3158024 | tf_op jit(solution)/shard_map/ppermute | solution.py:616
  93.9 16.3 %collective-permute-start.7 = (f32[1,129,8,128]{3,2,1,0:T(8,128)}, f32[1,129,8,128]{3,2,1,0:T(8,128)S(1)}, u32[]{:S(2)}, u32[]{:S(2)}) collective-permute-start(f32[1,129,8,128]{3,2,1,0:T(8,128)} %get-tuple-element.57), channel_id=1, source_target_pairs={{0,8},{1,33},{2,10},{3,35},{4,12},{5,37},{6,14},{7,39},{8,16},{9,4... | collective-permute-start | bytes 1585160 | tf_op jit(solution)/shard_map/ppermute | solution.py:616
  96.1 15.0 %collective-permute-start.8 = (f32[1,129,8,128]{3,2,1,0:T(8,128)}, f32[1,129,8,128]{3,2,1,0:T(8,128)S(1)}, u32[]{:S(2)}, u32[]{:S(2)}) collective-permute-start(f32[1,129,8,128]{3,2,1,0:T(8,128)} %get-tuple-element.58), channel_id=1, source_target_pairs={{0,24},{1,97},{2,26},{3,99},{4,28},{5,101},{6,30},{7,103},{8,0},{9... | collective-permute-start | bytes 1585160 | tf_op jit(solution)/shard_map/ppermute | solution.py:616
  110.3 0.9 copy-start.5
  111.1 0.8 copy-start.6
  116.0 1.0 copy-start.3
  116.0 1.3 copy-start.4
  126.0 2.2 %collective-permute-start.12 = (f32[4,36,8,128]{3,2,1,0:T(8,128)}, f32[4,36,8,128]{3,2,1,0:T(8,128)S(1)}, u32[]{:S(2)}, u32[]{:S(2)}) collective-permute-start(f32[4,36,8,128]{3,2,1,0:T(8,128)} %get-tuple-element.66), channel_id=1, source_target_pairs={{0,1},{1,0},{2,3},{3,2},{4,5},{5,4},{6,7},{7,6},{8,9},{9,8},{10,11... | collective-permute-start | bytes 1769480 | tf_op jit(solution)/shard_map/ppermute | solution.py:703
  130.0 10.7 %collective-permute-start.15 = (f32[36,8,128]{2,1,0:T(8,128)S(1)}, f32[36,8,128]{2,1,0:T(8,128)S(1)}, u32[]{:S(2)}, u32[]{:S(2)}) collective-permute-start(f32[36,8,128]{2,1,0:T(8,128)S(1)} %get-tuple-element.71), channel_id=1, source_target_pairs={{0,6},{1,7},{2,0},{3,1},{4,2},{5,3},{6,4},{7,5},{8,14},{9,15},{10,... | collective-permute-start | bytes 442376 | tf_op jit(solution)/shard_map/ppermute | solution.py:621
  134.1 8.3 %collective-permute-start.14 = (f32[36,8,128]{2,1,0:T(8,128)S(1)}, f32[36,8,128]{2,1,0:T(8,128)S(1)}, u32[]{:S(2)}, u32[]{:S(2)}) collective-permute-start(f32[36,8,128]{2,1,0:T(8,128)S(1)} %get-tuple-element.72), channel_id=1, source_target_pairs={{0,4},{1,5},{2,6},{3,7},{4,0},{5,1},{6,2},{7,3},{8,12},{9,13},{10,... | collective-permute-start | bytes 442376 | tf_op jit(solution)/shard_map/ppermute | solution.py:621
  134.5 9.9 %collective-permute-start.13 = (f32[36,8,128]{2,1,0:T(8,128)S(1)}, f32[36,8,128]{2,1,0:T(8,128)S(1)}, u32[]{:S(2)}, u32[]{:S(2)}) collective-permute-start(f32[36,8,128]{2,1,0:T(8,128)S(1)} %get-tuple-element.73), channel_id=1, source_target_pairs={{0,2},{1,3},{2,4},{3,5},{4,6},{5,7},{6,0},{7,1},{8,10},{9,11},{10,... | collective-permute-start | bytes 442376 | tf_op jit(solution)/shard_map/ppermute | solution.py:621
  140.7 3.7 %copy-start.7 = (f32[36,8,128]{2,1,0:T(8,128)}, f32[36,8,128]{2,1,0:T(8,128)S(1)}, u32[]{:S(2)}) copy-start(f32[36,8,128]{2,1,0:T(8,128)S(1)} %collective-permute-done.15.g3) | copy-start | bytes 442372
  142.4 2.0 %copy-start.8 = (f32[36,8,128]{2,1,0:T(8,128)}, f32[36,8,128]{2,1,0:T(8,128)S(1)}, u32[]{:S(2)}) copy-start(f32[36,8,128]{2,1,0:T(8,128)S(1)} %collective-permute-done.14.g2) | copy-start | bytes 442372
  144.4 0.7 copy-start.9

commit v2 on v1

--- a/solution.py
+++ b/solution.py
@@ -96,7 +96,7 @@
 ORDER = tuple(m for chunk in CHUNKS for m in chunk)
 
 
-def route_kernel(here, plan, leaf, table, labels, picked, scaled):
+def route(here, plan, leaf, table, labels, picked, scaled):
     bf16 = jnp.bfloat16
     cap = labels.shape[2]
     target = plan[...]
@@ -199,29 +199,19 @@
     return cap + 1
 
 
-def route(here, plan, leaf):
-    bins = plan.shape[0]
-    return pl.pallas_call(
-        route_kernel,
-        out_shape=(
-            jax.ShapeDtypeStruct((24, 128), i32),
-            jax.ShapeDtypeStruct((16, 8, 128), f32),
-        ),
-        in_specs=[SMEM, VMEM, VMEM],
-        out_specs=(VMEM, VMEM),
-        scratch_shapes=[pltpu.VMEM((128, 128), f32)] * 2,
-        name="route",
-    )(here, plan.reshape(bins // 128, 128), leaf.reshape(bins // 128, 128))
-
-
 GROUP = 16
 ENTRIES = 1152
 
 
-def expand_kernel(chunk, table, labels, pts, *refs):
-    outs = refs[:4]
-    held, all_pts = refs[4:6]
-    stage, bx, by, bz, sems, load_sems = refs[6:]
+def expand_kernel(chunk, *refs):
+    if chunk:
+        table, labels, pts, *refs = refs
+    else:
+        here, plan, leaf, pts, *refs = refs
+    outs, refs = refs[:4], refs[4:]
+    if not chunk:
+        listed, labels, *refs = refs
+    held, all_pts, stage, bx, by, bz, sems, load_sems, *refs = refs
     first = sum(len(c) for c in CHUNKS[:chunk])
     wide = len(CHUNKS[chunk])
     rows = outs[0].shape[1]
@@ -236,16 +226,26 @@
     ]
     for load in loads:
         load.start()
+    if not chunk:
+        table, picked, scaled, sem = refs
+        route(here, plan, leaf, listed, labels, picked, scaled)
+        copy = pltpu.make_async_copy(listed, table, sem)
+        copy.start()
+        copy.wait()
+
+    def look(n):
+        return table[n] if chunk else table[n >> 7, n & 127]
+
     for k in range(4):
         for n in range(wide):
             held[1 + (k * wide + n) * rows + cap] = labels[4 * (first + n) + k]
-    begin = table[2 * ENTRIES + 2 * chunk]
-    trips = table[2 * ENTRIES + 2 * chunk + 1]
+    begin = look(i32(2 * ENTRIES + 2 * chunk))
+    trips = look(i32(2 * ENTRIES + 2 * chunk + 1))
     for load in loads:
         load.wait()
 
     def fetch(g, u, bank):
-        line = table[begin + g * GROUP + u]
+        line = look(begin + g * GROUP + u)
         for axis in range(3):
             for h in range(2):
                 stage[bank, axis, h, pl.ds(u, 1), :] = all_pts[
@@ -264,7 +264,7 @@
 
     def consume(g, u, bank):
         base = begin + g * GROUP
-        line = table[base + u]
+        line = look(base + u)
         weighted, pair = [], []
         for h in range(2):
             lx = bx[bank, h, pl.ds(8 * u, 8), :]
@@ -291,7 +291,7 @@
             (((1,), (1,)), ((), ())),
             preferred_element_type=f32,
         )
-        held[table[base + (ENTRIES + u)]] = jnp.concatenate([res[:8], res[8:]], axis=1)
+        held[look(base + (ENTRIES + u))] = jnp.concatenate([res[:8], res[8:]], axis=1)
 
     pieces = 6 * GROUP // 8
     for u in range(GROUP):
@@ -327,13 +327,31 @@
         copy.wait()
 
 
-def expand(chunk, table, labels, pts, cap):
+def expand(chunk, routing, pts, cap):
     wide = len(CHUNKS[chunk])
+    out_shape = [jax.ShapeDtypeStruct((wide, cap + 1, 8, 128), f32)] * 4
+    out_specs = [ANY] * 4
+    scratch = []
+    if chunk:
+        in_specs = [SMEM, VMEM, ANY]
+    else:
+        in_specs = [SMEM, VMEM, VMEM, ANY]
+        out_shape += [
+            jax.ShapeDtypeStruct((24, 128), i32),
+            jax.ShapeDtypeStruct((16, 8, 128), f32),
+        ]
+        out_specs += [VMEM] * 2
+        scratch = [
+            pltpu.SMEM((24, 128), i32),
+            pltpu.VMEM((128, 128), f32),
+            pltpu.VMEM((128, 128), f32),
+            pltpu.SemaphoreType.DMA(()),
+        ]
     return pl.pallas_call(
         functools.partial(expand_kernel, chunk),
-        out_shape=[jax.ShapeDtypeStruct((wide, cap + 1, 8, 128), f32)] * 4,
-        in_specs=[SMEM, VMEM, ANY],
-        out_specs=[ANY] * 4,
+        out_shape=out_shape,
+        in_specs=in_specs,
+        out_specs=out_specs,
         scratch_shapes=[
             pltpu.VMEM((4 * wide * (cap + 1) + 1, 8, 128), f32),
             pltpu.VMEM(pts.shape, f32),
@@ -341,12 +359,13 @@
             *[pltpu.VMEM((2, 2, 8 * GROUP, 128), f32)] * 3,
             pltpu.SemaphoreType.DMA((4, wide)),
             pltpu.SemaphoreType.DMA((5,)),
+            *scratch,
         ],
         cost_estimate=pl.CostEstimate(
             flops=wide * (1 << 28), bytes_accessed=1 << 23, transcendentals=0
         ),
         name="expand",
-    )(table, labels, pts)
+    )(*routing, pts)
 
 
 def gather_kernel(wide, *refs):
@@ -507,23 +526,44 @@
 
 def levels_kernel(
     here, goal, boxes, a0, a1, a2, a3, p0c, p0s, p1c, p1s, both, rows, leaves, mine, other,
-    acc, upper, moved,
+    held, turns, lanes_in, rows_in, solved, acc, upper, moved, sems, out_sems,
 ):
+    count = leaves.shape[0]
+    sums = [
+        pltpu.make_async_copy(ref.at[pl.ds(0, count)], held.at[n], sems.at[n])
+        for n, ref in enumerate((a0, a1, a2, a3))
+    ]
+    maps = [
+        pltpu.make_async_copy(both, lanes_in, sems.at[4]),
+        pltpu.make_async_copy(rows, rows_in, sems.at[5]),
+    ]
+    angles = [
+        pltpu.make_async_copy(ref, turns.at[n], sems.at[6 + n])
+        for n, ref in enumerate((p0c, p0s, p1c, p1s))
+    ]
+    for copy in sums + maps + angles:
+        copy.start()
     acc[...] = jnp.zeros(acc.shape, f32)
     upper[...] = jnp.zeros(upper.shape, f32)
+    for copy in sums:
+        copy.wait()
     step = 16
     shape = (step, 8, 128)
     own = rows_of(shape) % 2 == lanes_of(shape) // 64
 
     def settle(n, carry):
         base = pl.multiple_of(n * step, step)
-        t = (a0[pl.ds(base, step)] + a1[pl.ds(base, step)]) + (
-            a2[pl.ds(base, step)] + a3[pl.ds(base, step)]
+        t = (held[0, pl.ds(base, step)] + held[1, pl.ds(base, step)]) + (
+            held[2, pl.ds(base, step)] + held[3, pl.ds(base, step)]
         )
-        leaves[pl.ds(base, step)] = jnp.where(own, t, swap_rows(pltpu.roll(t, 64, 2)))
+        solved[pl.ds(base, step)] = jnp.where(own, t, swap_rows(pltpu.roll(t, 64, 2)))
         return carry
 
-    lax.fori_loop(0, leaves.shape[0] // step, settle, 0)
+    lax.fori_loop(0, count // step, settle, 0)
+    done = [pltpu.make_async_copy(solved, leaves, out_sems.at[8])]
+    done[0].start()
+    for copy in maps + angles[:2]:
+        copy.wait()
 
     def spread(o, start, ref, spots):
         sums = [ref[spots[j]] + moved[o % 2, start + j] for j in range(8)]
@@ -532,13 +572,15 @@
 
     for o in range(8):
         for part in range(0, 32, 8):
-            t = jnp.stack([leaves[8 * (part + j) + o] for j in range(8)])
-            t = spin(t, p0c[o, part : part + 8], p0s[o, part : part + 8])
-            moved[o % 2, part : part + 8] = row_mix(lane_mix(t, both, o), rows, o // 4)
+            t = jnp.stack([solved[8 * (part + j) + o] for j in range(8)])
+            t = spin(t, turns[0, o, part : part + 8], turns[1, o, part : part + 8])
+            moved[o % 2, part : part + 8] = row_mix(lane_mix(t, lanes_in, o), rows_in, o // 4)
         for part in range(0, 32, 8):
             spread(o, part, acc, [goal[32 * o + part + j] for j in range(8)])
 
     apart = [here[2] * 4 * SEATS, (1 - here[2]) * 4 * SEATS]
+    for copy in angles[2:]:
+        copy.wait()
     for o in range(8):
         for part in range(0, 32, 8):
             tiles = []
@@ -546,23 +588,34 @@
                 p = 8 * (part + j) + o
                 owner = p // 32
                 tiles.append(acc[(owner // 2) * SEATS + p % 32 + apart[owner % 2]])
-            t = spin(jnp.stack(tiles), p1c[o, part : part + 8], p1s[o, part : part + 8])
-            moved[o % 2, part : part + 8] = lane_mix(t, both, o)
+            t = spin(
+                jnp.stack(tiles), turns[2, o, part : part + 8], turns[3, o, part : part + 8]
+            )
+            moved[o % 2, part : part + 8] = lane_mix(t, lanes_in, o)
         for part in range(0, 32, 8):
             spread(
                 o, part, upper,
                 [boxes[32 * o + part + j] + 32 * (o // 4) for j in range(8)],
             )
     for part in range(0, 32, 8):
-        t = row_mix(upper[part : part + 8], rows, 0) + row_mix(upper[32 + part : 40 + part], rows, 1)
+        t = row_mix(upper[part : part + 8], rows_in, 0)
+        t = t + row_mix(upper[32 + part : 40 + part], rows_in, 1)
         for j in range(8):
             q = part + j
             owner = q // 4
             acc[(owner // 2) * SEATS + 32 + q % 4 + apart[owner % 2]] = t[j]
     for k in range(4):
         z = (here[3] + k) % 4
-        mine[k] = acc[pl.ds(z * SEATS, SEATS)]
-        other[k] = acc[pl.ds((4 + z) * SEATS, SEATS)]
+        done += [
+            pltpu.make_async_copy(
+                acc.at[pl.ds((4 + z) * SEATS, SEATS)], other.at[k], out_sems.at[4 + k]
+            ),
+            pltpu.make_async_copy(acc.at[pl.ds(z * SEATS, SEATS)], mine.at[k], out_sems.at[k]),
+        ]
+    for copy in done[1:]:
+        copy.start()
+    for copy in done:
+        copy.wait()
 
 
 def close_kernel(g0, g1, g2, g3, ec, es, out_one, out_two):
@@ -641,15 +694,18 @@
 
     me = lax.axis_index("sfc")
     here = jnp.stack([me % 4, me // 4, rank % 2, rank // 2]).astype(i32)
-    table, labels = route(here, bin_plan[:, 0], bin_leaf)
-    table = table.reshape(-1)
     bins, _, width = bin_points.shape
     pts = jnp.transpose(bin_points.reshape(bins // 8, 8, 5, width // 128, 128), (2, 0, 3, 1, 4))
     pts = pts.reshape(-1, 128)
     arrived = []
+    routing = (here, bin_plan.reshape(bins // 128, 128), bin_leaf.reshape(bins // 128, 128))
     for c in range(len(CHUNKS)):
-        sent = expand(c, table, labels, pts, cap)
+        sent = expand(c, routing, pts, cap)
+        if not c:
+            *sent, table, labels = sent
+            table = table.reshape(-1)
         table = after(table, sent[0])
+        routing = (table, labels)
         moved = [sent[0]]
         for k in (2, 1, 3):
             moved.append(hop(sent[k], k, 0, groups))
@@ -688,12 +744,19 @@
     leaves, mine, other = pl.pallas_call(
         levels_kernel,
         out_shape=(tiles(leaf_count), tiles(4, SEATS), tiles(4, SEATS)),
-        in_specs=[SMEM] * 3 + [VMEM] * 10,
-        out_specs=(VMEM,) * 3,
+        in_specs=[SMEM] * 3 + [ANY] * 10,
+        out_specs=(ANY,) * 3,
         scratch_shapes=[
+            pltpu.VMEM((4, leaf_count, 8, 128), f32),
+            pltpu.VMEM((4, 8, 32, 8, 128), f32),
+            pltpu.VMEM((4, 256, 256), jnp.bfloat16),
+            pltpu.VMEM((2, 8, 8, 128), f32),
+            pltpu.VMEM((leaf_count, 8, 128), f32),
             pltpu.VMEM((8 * SEATS, 8, 128), f32),
             pltpu.VMEM((64, 8, 128), f32),
             pltpu.VMEM((2, 32, 8, 128), f32),
+            pltpu.SemaphoreType.DMA((10,)),
+            pltpu.SemaphoreType.DMA((9,)),
         ],
         name="levels",
     )(

time: 148 us -> 146 us (0.986)
  Pallas kernels: 78 us -> 75.5 us
    pallas_call x4 -> x3, Pallas kernels: 45.4 us -> 43.5 us  [expand(): pl.pallas_call(functools.partial(expand_kernel, chunk), out_shape=out_sha...]
  transfers between devices with their start and end apart: 16 -> 16, of which waited for: 7 -> 7; matrix products, arithmetic and copies ran while one was open for 2% -> 2% of each run, Pallas kernels for 37% -> 38%
where the time goes in v2:
time: 146 us; the launch traced here: 145 us
  Pallas kernels  75.5 us (52%)
  waiting for transfers between devices  31.4 us (22%)
  starting transfers between devices  26 us (18%)
  local copies, waits for them, and re-layouts  6.41 us (4%)
  other arithmetic  4.4 us (3%)
    pallas_call x3, Pallas kernels, expand(): pl.pallas_call(functools.partial(expand_kernel, chunk), out_shape=out_sha...  43.5 us
    ppermute x12, waiting for transfers between devices, hop(): return lax.ppermute(x, ('sfc', 'grp'), pairs)  20.7 us
    ppermute x12, starting transfers between devices, hop(): return lax.ppermute(x, ('sfc', 'grp'), pairs)  20 us
    pallas_call x3, Pallas kernels, gather(): pl.pallas_call(functools.partial(gather_kernel, wide), out_shape=[jax.Sha...  16.2 us
    ppermute x3, waiting for transfers between devices, around(): return lax.ppermute(x, 'grp', pairs)  8.44 us
    pallas_call x1, Pallas kernels, per_device(): pl.pallas_call(levels_kernel, out_shape=(tiles(leaf_count), tiles(4, SEAT...  8.06 us
    ppermute x3, starting transfers between devices, around(): return lax.ppermute(x, 'grp', pairs)  5.9 us
    pallas_call x1, Pallas kernels, per_device(): make_phases(here, slots, boxes, parent_cone[0], box_cone[0], jnp.cos(angl...  5.75 us
  transfers between devices with their start and end apart: 16, of which 7 were waited for; matrix products, arithmetic and copies ran while one was open for 2% of the time, Pallas kernels for 38%

profile of v2, /device:TPU:0, one launch (start us, length us, event | category | flops | bytes accessed | tf_op | source)
XLA Modules:
  0.0 144.6 jit_solution(14742514141607990610)
XLA Ops:
  0.7 0.6 pad_add_fusion.refs_0_.here
  1.3 10.6 %expand.3 = (f32[1,129,8,128]{3,2,1,0:T(8,128)}, f32[1,129,8,128]{3,2,1,0:T(8,128)}, f32[1,129,8,128]{3,2,1,0:T(8,128)}, f32[1,129,8,128]{3,2,1,0:T(8,128)}, s32[24,128]{1,0:T(8,128)}, /*index=5*/f32[16,8,128]{2,1,0:T(8,128)}) custom-call(s32[4]{0:T(128)} %pad_add_fusion.refs_0_.here, s32[8,128]{1,0:T(8,128)} %bitcast.48, s32[8,128]{1,0:T(8,128)} %bitcast.49, ...), custom_call_target="tpu_custom_call" | custom-call | flops 268435456 | bytes 8388608 | tf_op jit(solution)/shard_map/expand/pallas_call | solution.py:350
  11.8 2.8 %collective-permute-start = (f32[1,129,8,128]{3,2,1,0:T(8,128)}, f32[1,129,8,128]{3,2,1,0:T(8,128)}, u32[]{:S(2)}, u32[]{:S(2)}) collective-permute-start(f32[1,129,8,128]{3,2,1,0:T(8,128)} %get-tuple-element.47), channel_id=1, source_target_pairs={{0,16},{1,65},{2,18},{3,67},{4,20},{5,69},{6,22},{7,71},{8,24},{9,... | collective-permute-start | bytes 1585160 | tf_op jit(solution)/shard_map/ppermute | solution.py:669
  14.6 21.8 %expand.4 = (f32[2,129,8,128]{3,2,1,0:T(8,128)}, f32[2,129,8,128]{3,2,1,0:T(8,128)}, f32[2,129,8,128]{3,2,1,0:T(8,128)}, f32[2,129,8,128]{3,2,1,0:T(8,128)}) custom-call(s32[3072]{0:T(1024)} %bitcast.46, f32[16,8,128]{2,1,0:T(8,128)} %get-tuple-element.40.refs_1_, f32[10240,128]{1,0:T(8,128)} %bitcast.44), custom_call_target="tpu_custom_call" | custom-call | flops 536870912 | bytes 8388608 | tf_op jit(solution)/shard_map/expand/pallas_call | solution.py:350
  36.4 0.1 collective-permute-start.3
  36.5 2.8 %collective-permute-start.4 = (f32[2,129,8,128]{3,2,1,0:T(8,128)}, f32[2,129,8,128]{3,2,1,0:T(8,128)S(1)}, u32[]{:S(2)}, u32[]{:S(2)}) collective-permute-start(f32[2,129,8,128]{3,2,1,0:T(8,128)} %get-tuple-element.52), channel_id=1, source_target_pairs={{0,8},{1,33},{2,10},{3,35},{4,12},{5,37},{6,14},{7,39},{8,16},{9,4... | collective-permute-start | bytes 3170312 | tf_op jit(solution)/shard_map/ppermute | solution.py:669
  39.4 0.5 collective-permute-start.5
  39.8 1.6 %collective-permute-start.1 = (f32[1,129,8,128]{3,2,1,0:T(8,128)}, f32[1,129,8,128]{3,2,1,0:T(8,128)}, u32[]{:S(2)}, u32[]{:S(2)}) collective-permute-start(f32[1,129,8,128]{3,2,1,0:T(8,128)} %get-tuple-element.48), channel_id=1, source_target_pairs={{0,8},{1,33},{2,10},{3,35},{4,12},{5,37},{6,14},{7,39},{8,16},{9,4... | collective-permute-start | bytes 1585160 | tf_op jit(solution)/shard_map/ppermute | solution.py:669
  41.4 1.7 %collective-permute-start.2 = (f32[1,129,8,128]{3,2,1,0:T(8,128)}, f32[1,129,8,128]{3,2,1,0:T(8,128)}, u32[]{:S(2)}, u32[]{:S(2)}) collective-permute-start(f32[1,129,8,128]{3,2,1,0:T(8,128)} %get-tuple-element.49), channel_id=1, source_target_pairs={{0,24},{1,97},{2,26},{3,99},{4,28},{5,101},{6,30},{7,103},{8,0},{9... | collective-permute-start | bytes 1585160 | tf_op jit(solution)/shard_map/ppermute | solution.py:669
  43.1 11.2 %expand.5 = (f32[1,129,8,128]{3,2,1,0:T(8,128)}, f32[1,129,8,128]{3,2,1,0:T(8,128)}, f32[1,129,8,128]{3,2,1,0:T(8,128)}, f32[1,129,8,128]{3,2,1,0:T(8,128)}) custom-call(s32[3072]{0:T(1024)} %bitcast.47, f32[16,8,128]{2,1,0:T(8,128)} %get-tuple-element.40.refs_1_, f32[10240,128]{1,0:T(8,128)} %bitcast.45), custom_call_target="tpu_custom_call" | custom-call | flops 268435456 | bytes 8388608 | tf_op jit(solution)/shard_map/expand/pallas_call | solution.py:350
  54.3 15.7 %collective-permute-done.1.refs_2_ = f32[1,129,8,128]{3,2,1,0:T(8,128)} collective-permute-done((f32[1,129,8,128]{3,2,1,0:T(8,128)}, f32[1,129,8,128]{3,2,1,0:T(8,128)}, u32[]{:S(2)}, u32[]{:S(2)}) %collective-permute-start.1) | collective-permute-done | bytes 528416 | tf_op jit(solution)/shard_map/ppermute | solution.py:669
  70.0 0.2 collective-permute-start.6
  70.2 4.4 %gather.3 = f32[257,8,128]{2,1,0:T(8,128)} custom-call(f32[1,129,8,128]{3,2,1,0:T(8,128)} %get-tuple-element.46.refs_0_, f32[1,129,8,128]{3,2,1,0:T(8,128)} %collective-permute-done.refs_1_, f32[1,129,8,128]{3,2,1,0:T(8,128)} %collective-permute-done.1.refs_2_, f32[1,129,8,128]{3,2,1,0:T(8,128)} %collective-permute-done.2.refs_3_), custom_call_target="tpu_custom_call" | custom-call | flops 67108864 | bytes 4194304 | tf_op jit(solution)/shard_map/gather/pallas_call | solution.py:406
  74.7 0.0 copy-start.10
  74.7 0.0 copy-start.11
  74.7 0.0 copy-start.12
  74.7 5.1 %collective-permute-start.10 = (f32[257,8,128]{2,1,0:T(8,128)}, f32[257,8,128]{2,1,0:T(8,128)}, u32[]{:S(2)}, u32[]{:S(2)}) collective-permute-start(f32[257,8,128]{2,1,0:T(8,128)} %gather.3), channel_id=1, source_target_pairs={{0,64},{1,17},{2,66},{3,19},{4,68},{5,21},{6,70},{7,23},{8,72},{9,... | collective-permute-start | bytes 3158024 | tf_op jit(solution)/shard_map/ppermute | solution.py:669
  79.8 1.0 copy-done
  80.8 0.4 copy-done.1
  81.2 1.0 copy-done.2
  82.2 7.8 %gather.4 = (f32[257,8,128]{2,1,0:T(8,128)}, f32[257,8,128]{2,1,0:T(8,128)}) custom-call(f32[2,129,8,128]{3,2,1,0:T(8,128)} %get-tuple-element.50.refs_0_, f32[2,129,8,128]{3,2,1,0:T(8,128)} %copy-done, f32[2,129,8,128]{3,2,1,0:T(8,128)} %copy-done.1, f32[2,129,8,128]{3,2,1,0:T(8,128)} %copy-done.2), custom_call_target="tpu_custom_call" | custom-call | flops 134217728 | bytes 8388608 | tf_op jit(solution)/shard_map/gather/pallas_call | solution.py:406
  89.9 0.1 collective-permute-start.11
  90.0 2.0 %collective-permute-start.9 = (f32[257,8,128]{2,1,0:T(8,128)}, f32[257,8,128]{2,1,0:T(8,128)S(1)}, u32[]{:S(2)}, u32[]{:S(2)}) collective-permute-start(f32[257,8,128]{2,1,0:T(8,128)} %get-tuple-element.54), channel_id=1, source_target_pairs={{0,32},{1,9},{2,34},{3,11},{4,36},{5,13},{6,38},{7,15},{8,40},{9,1... | collective-permute-start | bytes 3158024 | tf_op jit(solution)/shard_map/ppermute | solution.py:669
  92.0 2.2 %collective-permute-start.7 = (f32[1,129,8,128]{3,2,1,0:T(8,128)}, f32[1,129,8,128]{3,2,1,0:T(8,128)S(1)}, u32[]{:S(2)}, u32[]{:S(2)}) collective-permute-start(f32[1,129,8,128]{3,2,1,0:T(8,128)} %get-tuple-element.57), channel_id=1, source_target_pairs={{0,8},{1,33},{2,10},{3,35},{4,12},{5,37},{6,14},{7,39},{8,16},{9,4... | collective-permute-start | bytes 1585160 | tf_op jit(solution)/shard_map/ppermute | solution.py:669
  94.2 1.0 collective-permute-start.8
  95.3 0.6 reshape.81.boxes
  95.9 0.6 reshape.80.slots
  96.6 0.1 multiply_bitcast_fusion.1
  96.6 1.9 %fusion = (f32[16,4,8,128]{3,2,1,0:T(8,128)}, f32[16,4,8,128]{3,2,1,0:T(8,128)}) fusion(f32[4,8,128]{2,1,0:T(8,128)S(1)} %copy-done.10, f32[16]{0:T(128)S(1)} %get-tuple-element.78, f32[4,8,128]{2,1,0:T(8,128)S(1)} %copy-done.11, f32[16]{0:T(128)S(1)} %get-tuple-element.79, f32[4,8,128]{2,1,0:T(8,128)S(1)} %copy-done.12, f32[16]{0:T(128)S(1)} %get-tuple-element.77), kind=kLoop, calls=%fused_computation.1 | loop fusion | flops 393216 | bytes 573632 | tf_op jit(solution)/shard_map/sin | solution.py:732
  98.5 5.8 %phases.1 = (f32[8,32,8,128]{3,2,1,0:T(8,128)}, f32[8,32,8,128]{3,2,1,0:T(8,128)}, f32[8,32,8,128]{3,2,1,0:T(8,128)}, f32[8,32,8,128]{3,2,1,0:T(8,128)}, f32[36,...) custom-call(s32[4]{0:T(128)} %pad_add_fusion.refs_0_.here, s32[256]{0:T(256)} %reshape.80.slots, ...), custom_call_target="tpu_custom_call" | custom-call | tf_op jit(solution)/shard_map/phases/pallas_call | solution.py:731
  104.3 4.0 %collective-permute-done.7.refs_2_ = f32[1,129,8,128]{3,2,1,0:T(8,128)S(1)} collective-permute-done((f32[1,129,8,128]{3,2,1,0:T(8,128)}, f32[1,129,8,128]{3,2,1,0:T(8,128)S(1)}, u32[]{:S(2)}, u32[]{:S(2)}) %collective-permute-start.7) | collective-permute-done | bytes 528416 | tf_op jit(solution)/shard_map/ppermute | solution.py:669
  108.3 0.9 collective-permute-done.8.refs_3_
  109.3 0.8 copy-done.6
  110.1 4.0 %gather.5.a0 = f32[257,8,128]{2,1,0:T(8,128)} custom-call(f32[1,129,8,128]{3,2,1,0:T(8,128)} %get-tuple-element.55.refs_0_, f32[1,129,8,128]{3,2,1,0:T(8,128)} %collective-permute-done.6.refs_1_, f32[1,129,8,128]{3,2,1,0:T(8,128)} %copy-done.5, f32[1,129,8,128]{3,2,1,0:T(8,128)} %copy-done.6), custom_call_target="tpu_custom_call" | custom-call | flops 67108864 | bytes 4194304 | tf_op jit(solution)/shard_map/gather/pallas_call | solution.py:406
  114.1 1.0 copy-done.3
  115.1 0.3 copy-done.4
  115.4 8.1 %levels.1 = (f32[256,8,128]{2,1,0:T(8,128)}, f32[4,36,8,128]{3,2,1,0:T(8,128)}, f32[4,36,8,128]{3,2,1,0:T(8,128)}) custom-call(s32[4]{0:T(128)} %pad_add_fusion.refs_0_.here, s32[256]{0:T(256)} %get-tuple-element.45.goal, s32[256]{0:T(256)} %reshape.81.boxes, f32[257,8,128]{2,1,0:T(8,128)} %gather.5.a0, f32[257,8,128]{2,1,0:T(8,128)} %copy-done.4, ...), custom_call_target="tpu_custom_call" | custom-call | tf_op jit(solution)/shard_map/levels/pallas_call | solution.py:744
  123.5 0.1 collective-permute-start.12
  123.6 2.2 %collective-permute-done.12 = f32[4,36,8,128]{3,2,1,0:T(8,128)S(1)} collective-permute-done((f32[4,36,8,128]{3,2,1,0:T(8,128)}, f32[4,36,8,128]{3,2,1,0:T(8,128)S(1)}, u32[]{:S(2)}, u32[]{:S(2)}) %collective-permute-start.12) | collective-permute-done | bytes 589856 | tf_op jit(solution)/shard_map/ppermute | solution.py:766
  125.8 1.8 %fusion.2 = (f32[36,8,128]{2,1,0:T(8,128)S(1)}, f32[36,8,128]{2,1,0:T(8,128)S(1)}, f32[36,8,128]{2,1,0:T(8,128)S(1)}, f32[36,8,128]{2,1,0:T(8,128)}) fusion(f32[4,36,8,128]{3,2,1,0:T(8,128)S(1)} %collective-permute-done.12, f32[4,36,8,128]{3,2,1,0:T(8,128)} %get-tuple-element.65), kind=kLoop, calls=%fused_computation.4 | loop fusion | flops 147456 | bytes 1769472 | tf_op jit(solution)/shard_map/add | solution.py:767
  127.6 4.1 %collective-permute-start.15 = (f32[36,8,128]{2,1,0:T(8,128)S(1)}, f32[36,8,128]{2,1,0:T(8,128)S(1)}, u32[]{:S(2)}, u32[]{:S(2)}) collective-permute-start(f32[36,8,128]{2,1,0:T(8,128)S(1)} %get-tuple-element.71), channel_id=1, source_target_pairs={{0,6},{1,7},{2,0},{3,1},{4,2},{5,3},{6,4},{7,5},{8,14},{9,15},{10,... | collective-permute-start | bytes 442376 | tf_op jit(solution)/shard_map/ppermute | solution.py:674
  131.7 0.4 collective-permute-start.14
  132.1 1.4 collective-permute-start.13
  133.5 4.7 %collective-permute-done.15.g3 = f32[36,8,128]{2,1,0:T(8,128)S(1)} collective-permute-done((f32[36,8,128]{2,1,0:T(8,128)S(1)}, f32[36,8,128]{2,1,0:T(8,128)S(1)}, u32[]{:S(2)}, u32[]{:S(2)}) %collective-permute-start.15) | collective-permute-done | bytes 147488 | tf_op jit(solution)/shard_map/ppermute | solution.py:674
  138.3 1.7 %collective-permute-done.14.g2 = f32[36,8,128]{2,1,0:T(8,128)S(1)} collective-permute-done((f32[36,8,128]{2,1,0:T(8,128)S(1)}, f32[36,8,128]{2,1,0:T(8,128)S(1)}, u32[]{:S(2)}, u32[]{:S(2)}) %collective-permute-start.14) | collective-permute-done | bytes 147488 | tf_op jit(solution)/shard_map/ppermute | solution.py:674
  140.0 2.0 %collective-permute-done.13.g1 = f32[36,8,128]{2,1,0:T(8,128)S(1)} collective-permute-done((f32[36,8,128]{2,1,0:T(8,128)S(1)}, f32[36,8,128]{2,1,0:T(8,128)S(1)}, u32[]{:S(2)}, u32[]{:S(2)}) %collective-permute-start.13) | collective-permute-done | bytes 147488 | tf_op jit(solution)/shard_map/ppermute | solution.py:674
  142.0 0.7 copy-done.9
  142.6 1.9 %close.1 = (f32[32,8,128]{2,1,0:T(8,128)}, f32[4,8,128]{2,1,0:T(8,128)}) custom-call(f32[36,8,128]{2,1,0:T(8,128)} %get-tuple-element.74.g0, f32[36,8,128]{2,1,0:T(8,128)} %copy-done.9, f32[36,8,128]{2,1,0:T(8,128)} %copy-done.8, f32[36,8,128]{2,1,0:T(8,128)} %copy-done.7, f32[36,8,128]{2,1,0:T(8,128)} %get-tuple-element.67.ec, ...), custom_call_target="tpu_custom_call" | custom-call | tf_op jit(solution)/shard_map/close/pallas_call | solution.py:769
  (31 shorter events, 0.1 us)
Async XLA Ops:
  11.8 29.5 %collective-permute-start = (f32[1,129,8,128]{3,2,1,0:T(8,128)}, f32[1,129,8,128]{3,2,1,0:T(8,128)}, u32[]{:S(2)}, u32[]{:S(2)}) collective-permute-start(f32[1,129,8,128]{3,2,1,0:T(8,128)} %get-tuple-element.47), channel_id=1, source_target_pairs={{0,16},{1,65},{2,18},{3,67},{4,20},{5,69},{6,22},{7,71},{8,24},{9,... | collective-permute-start | bytes 1585160 | tf_op jit(solution)/shard_map/ppermute | solution.py:669
  36.4 43.4 %collective-permute-start.3 = (f32[2,129,8,128]{3,2,1,0:T(8,128)}, f32[2,129,8,128]{3,2,1,0:T(8,128)S(1)}, u32[]{:S(2)}, u32[]{:S(2)}) collective-permute-start(f32[2,129,8,128]{3,2,1,0:T(8,128)} %get-tuple-element.51), channel_id=1, source_target_pairs={{0,16},{1,65},{2,18},{3,67},{4,20},{5,69},{6,22},{7,71},{8,24},{9,... | collective-permute-start | bytes 3170312 | tf_op jit(solution)/shard_map/ppermute | solution.py:669
  36.5 43.3 %collective-permute-start.4 = (f32[2,129,8,128]{3,2,1,0:T(8,128)}, f32[2,129,8,128]{3,2,1,0:T(8,128)S(1)}, u32[]{:S(2)}, u32[]{:S(2)}) collective-permute-start(f32[2,129,8,128]{3,2,1,0:T(8,128)} %get-tuple-element.52), channel_id=1, source_target_pairs={{0,8},{1,33},{2,10},{3,35},{4,12},{5,37},{6,14},{7,39},{8,16},{9,4... | collective-permute-start | bytes 3170312 | tf_op jit(solution)/shard_map/ppermute | solution.py:669
  39.4 40.5 %collective-permute-start.5 = (f32[2,129,8,128]{3,2,1,0:T(8,128)}, f32[2,129,8,128]{3,2,1,0:T(8,128)S(1)}, u32[]{:S(2)}, u32[]{:S(2)}) collective-permute-start(f32[2,129,8,128]{3,2,1,0:T(8,128)} %get-tuple-element.53), channel_id=1, source_target_pairs={{0,24},{1,97},{2,26},{3,99},{4,28},{5,101},{6,30},{7,103},{8,0},{9... | collective-permute-start | bytes 3170312 | tf_op jit(solution)/shard_map/ppermute | solution.py:669
  39.8 30.2 %collective-permute-start.1 = (f32[1,129,8,128]{3,2,1,0:T(8,128)}, f32[1,129,8,128]{3,2,1,0:T(8,128)}, u32[]{:S(2)}, u32[]{:S(2)}) collective-permute-start(f32[1,129,8,128]{3,2,1,0:T(8,128)} %get-tuple-element.48), channel_id=1, source_target_pairs={{0,8},{1,33},{2,10},{3,35},{4,12},{5,37},{6,14},{7,39},{8,16},{9,4... | collective-permute-start | bytes 1585160 | tf_op jit(solution)/shard_map/ppermute | solution.py:669
  41.4 28.8 %collective-permute-start.2 = (f32[1,129,8,128]{3,2,1,0:T(8,128)}, f32[1,129,8,128]{3,2,1,0:T(8,128)}, u32[]{:S(2)}, u32[]{:S(2)}) collective-permute-start(f32[1,129,8,128]{3,2,1,0:T(8,128)} %get-tuple-element.49), channel_id=1, source_target_pairs={{0,24},{1,97},{2,26},{3,99},{4,28},{5,101},{6,30},{7,103},{8,0},{9... | collective-permute-start | bytes 1585160 | tf_op jit(solution)/shard_map/ppermute | solution.py:669
  70.0 24.3 %collective-permute-start.6 = (f32[1,129,8,128]{3,2,1,0:T(8,128)}, f32[1,129,8,128]{3,2,1,0:T(8,128)}, u32[]{:S(2)}, u32[]{:S(2)}) collective-permute-start(f32[1,129,8,128]{3,2,1,0:T(8,128)} %get-tuple-element.56), channel_id=1, source_target_pairs={{0,16},{1,65},{2,18},{3,67},{4,20},{5,69},{6,22},{7,71},{8,24},{9,... | collective-permute-start | bytes 1585160 | tf_op jit(solution)/shard_map/ppermute | solution.py:669
  74.6 20.6 %copy-start.13 = (s32[1,8,32]{2,1,0:T(8,128)S(1)}, s32[1,8,32]{2,1,0:T(8,128)}, u32[]{:S(2)}) copy-start(s32[1,8,32]{2,1,0:T(8,128)} %param.15) | copy-start | bytes 3076
  74.7 21.3 %copy-start.14 = (s32[1,8,32]{2,1,0:T(8,128)S(1)}, s32[1,8,32]{2,1,0:T(8,128)}, u32[]{:S(2)}) copy-start(s32[1,8,32]{2,1,0:T(8,128)} %param.14) | copy-start | bytes 3076
  74.7 21.9 %copy-start.15 = (f32[16,2]{0,1:T(2,128)S(1)}, f32[16,2]{0,1:T(2,128)}, u32[]{:S(2)}) copy-start(f32[16,2]{0,1:T(2,128)} %param.18) | copy-start | bytes 388
  74.7 21.9 %copy-start.10 = (f32[4,8,128]{2,1,0:T(8,128)S(1)}, f32[4,8,128]{2,1,0:T(8,128)}, u32[]{:S(2)}) copy-start(f32[4,8,128]{2,1,0:T(8,128)} %constant.71) | copy-start | bytes 49156
  74.7 21.9 %copy-start.11 = (f32[4,8,128]{2,1,0:T(8,128)S(1)}, f32[4,8,128]{2,1,0:T(8,128)}, u32[]{:S(2)}) copy-start(f32[4,8,128]{2,1,0:T(8,128)} %constant.69) | copy-start | bytes 49156
  74.7 21.9 %copy-start.12 = (f32[4,8,128]{2,1,0:T(8,128)S(1)}, f32[4,8,128]{2,1,0:T(8,128)}, u32[]{:S(2)}) copy-start(f32[4,8,128]{2,1,0:T(8,128)} %constant.67) | copy-start | bytes 49156
  74.7 39.4 %collective-permute-start.10 = (f32[257,8,128]{2,1,0:T(8,128)}, f32[257,8,128]{2,1,0:T(8,128)}, u32[]{:S(2)}, u32[]{:S(2)}) collective-permute-start(f32[257,8,128]{2,1,0:T(8,128)} %gather.3), channel_id=1, source_target_pairs={{0,64},{1,17},{2,66},{3,19},{4,68},{5,21},{6,70},{7,23},{8,72},{9,... | collective-permute-start | bytes 3158024 | tf_op jit(solution)/shard_map/ppermute | solution.py:669
  79.8 1.0 copy-start
  79.8 1.4 copy-start.1
  81.2 1.0 copy-start.2
  89.9 24.2 %collective-permute-start.11 = (f32[257,8,128]{2,1,0:T(8,128)}, f32[257,8,128]{2,1,0:T(8,128)S(1)}, u32[]{:S(2)}, u32[]{:S(2)}) collective-permute-start(f32[257,8,128]{2,1,0:T(8,128)} %get-tuple-element.59), channel_id=1, source_target_pairs={{0,96},{1,25},{2,98},{3,27},{4,100},{5,29},{6,102},{7,31},{8,104},... | collective-permute-start | bytes 3158024 | tf_op jit(solution)/shard_map/ppermute | solution.py:669
  90.0 24.1 %collective-permute-start.9 = (f32[257,8,128]{2,1,0:T(8,128)}, f32[257,8,128]{2,1,0:T(8,128)S(1)}, u32[]{:S(2)}, u32[]{:S(2)}) collective-permute-start(f32[257,8,128]{2,1,0:T(8,128)} %get-tuple-element.54), channel_id=1, source_target_pairs={{0,32},{1,9},{2,34},{3,11},{4,36},{5,13},{6,38},{7,15},{8,40},{9,1... | collective-permute-start | bytes 3158024 | tf_op jit(solution)/shard_map/ppermute | solution.py:669
  92.0 16.3 %collective-permute-start.7 = (f32[1,129,8,128]{3,2,1,0:T(8,128)}, f32[1,129,8,128]{3,2,1,0:T(8,128)S(1)}, u32[]{:S(2)}, u32[]{:S(2)}) collective-permute-start(f32[1,129,8,128]{3,2,1,0:T(8,128)} %get-tuple-element.57), channel_id=1, source_target_pairs={{0,8},{1,33},{2,10},{3,35},{4,12},{5,37},{6,14},{7,39},{8,16},{9,4... | collective-permute-start | bytes 1585160 | tf_op jit(solution)/shard_map/ppermute | solution.py:669
  94.2 15.0 %collective-permute-start.8 = (f32[1,129,8,128]{3,2,1,0:T(8,128)}, f32[1,129,8,128]{3,2,1,0:T(8,128)S(1)}, u32[]{:S(2)}, u32[]{:S(2)}) collective-permute-start(f32[1,129,8,128]{3,2,1,0:T(8,128)} %get-tuple-element.58), channel_id=1, source_target_pairs={{0,24},{1,97},{2,26},{3,99},{4,28},{5,101},{6,30},{7,103},{8,0},{9... | collective-permute-start | bytes 1585160 | tf_op jit(solution)/shard_map/ppermute | solution.py:669
  108.3 0.9 copy-start.5
  109.3 0.8 copy-start.6
  114.1 1.0 copy-start.3
  114.1 1.3 copy-start.4
  123.5 2.3 %collective-permute-start.12 = (f32[4,36,8,128]{3,2,1,0:T(8,128)}, f32[4,36,8,128]{3,2,1,0:T(8,128)S(1)}, u32[]{:S(2)}, u32[]{:S(2)}) collective-permute-start(f32[4,36,8,128]{3,2,1,0:T(8,128)} %get-tuple-element.66), channel_id=1, source_target_pairs={{0,1},{1,0},{2,3},{3,2},{4,5},{5,4},{6,7},{7,6},{8,9},{9,8},{10,11... | collective-permute-start | bytes 1769480 | tf_op jit(solution)/shard_map/ppermute | solution.py:766
  127.6 10.6 %collective-permute-start.15 = (f32[36,8,128]{2,1,0:T(8,128)S(1)}, f32[36,8,128]{2,1,0:T(8,128)S(1)}, u32[]{:S(2)}, u32[]{:S(2)}) collective-permute-start(f32[36,8,128]{2,1,0:T(8,128)S(1)} %get-tuple-element.71), channel_id=1, source_target_pairs={{0,6},{1,7},{2,0},{3,1},{4,2},{5,3},{6,4},{7,5},{8,14},{9,15},{10,... | collective-permute-start | bytes 442376 | tf_op jit(solution)/shard_map/ppermute | solution.py:674
  131.7 8.3 %collective-permute-start.14 = (f32[36,8,128]{2,1,0:T(8,128)S(1)}, f32[36,8,128]{2,1,0:T(8,128)S(1)}, u32[]{:S(2)}, u32[]{:S(2)}) collective-permute-start(f32[36,8,128]{2,1,0:T(8,128)S(1)} %get-tuple-element.72), channel_id=1, source_target_pairs={{0,4},{1,5},{2,6},{3,7},{4,0},{5,1},{6,2},{7,3},{8,12},{9,13},{10,... | collective-permute-start | bytes 442376 | tf_op jit(solution)/shard_map/ppermute | solution.py:674
  132.1 9.9 %collective-permute-start.13 = (f32[36,8,128]{2,1,0:T(8,128)S(1)}, f32[36,8,128]{2,1,0:T(8,128)S(1)}, u32[]{:S(2)}, u32[]{:S(2)}) collective-permute-start(f32[36,8,128]{2,1,0:T(8,128)S(1)} %get-tuple-element.73), channel_id=1, source_target_pairs={{0,2},{1,3},{2,4},{3,5},{4,6},{5,7},{6,0},{7,1},{8,10},{9,11},{10,... | collective-permute-start | bytes 442376 | tf_op jit(solution)/shard_map/ppermute | solution.py:674
  138.3 3.7 %copy-start.7 = (f32[36,8,128]{2,1,0:T(8,128)}, f32[36,8,128]{2,1,0:T(8,128)S(1)}, u32[]{:S(2)}) copy-start(f32[36,8,128]{2,1,0:T(8,128)S(1)} %collective-permute-done.15.g3) | copy-start | bytes 442372
  140.0 2.0 %copy-start.8 = (f32[36,8,128]{2,1,0:T(8,128)}, f32[36,8,128]{2,1,0:T(8,128)S(1)}, u32[]{:S(2)}) copy-start(f32[36,8,128]{2,1,0:T(8,128)S(1)} %collective-permute-done.14.g2) | copy-start | bytes 442372
  142.0 0.7 copy-start.9
